TPU v7x, 32 devices: a whole 2x2x4 slice. The times are simulated.
32 devices in a mesh: lon: 8 (over z, y), lev: 4 (over x, core).
Axes of the slice: x: 2, y: 2, z: 4, core: 2. Of those that a mesh axis runs over, the one named last changes fastest.
Arguments:
- column_old: float32 [70, 262144], P(None, ('lon', 'lev')), may hold values from -6 to 6
- coupling: float32 [69, 262144], P(None, ('lon', 'lev')), may hold values from 7.5 to 120, as said below
- sea_temp: float32 [262144], P(('lon', 'lev')), may hold values from -6 to 6
- land_mask: int32 [262144], P(('lon', 'lev')), may hold values from 0 to 1, as said below
- tile_weight: float32 [9, 262144], P(None, ('lon', 'lev')), may hold values from 0.05 to 1
- tile_coeff: float32 [9, 262144], P(None, ('lon', 'lev')), may hold values from 0.2 to 5
- tile_capacity: float32 [9, 262144], P(None, ('lon', 'lev')), may hold values from 0.5 to 5
- tile_conduct: float32 [9, 262144], P(None, ('lon', 'lev')), may hold values from 0.1 to 2
- tile_old: float32 [9, 262144], P(None, ('lon', 'lev')), may hold values from -6 to 6
- tile_forcing: float32 [9, 262144], P(None, ('lon', 'lev')), may hold values from -12 to 12
Outputs:
- column_temp: float32 [70, 262144], P(None, ('lon', 'lev'))
- tile_temp: float32 [9, 262144], P(None, ('lon', 'lev'))
Inputs may be any that keep to these rules, and one draw needn't show every extreme that they name: `land_mask`: 1 marks a land column, 0 an ocean column. `coupling`: positive.
All inputs are finite; a program needn't handle non-finite values.
Results may differ from a plain program's by a relative error of at most 0.0001.
Values sent between devices are 32-bit elements; how exact they have to be, the bound alone decides.
No kernel may reach another device: no remote copies, remote signals or barrier semaphores. Data moves between devices by JAX's collectives and lax.ppermute only.
A program may use at most 64 MiB of HBM per device.

v0:
```python
import jax
import jax.numpy as jnp
from jax import lax
from jax.sharding import PartitionSpec as P

ITERS = 8


HIGH = lax.Precision.HIGHEST


def extended(block, sides, width):
    for axis, dim in sides:
        count = lax.axis_size(axis)
        forward = [(i, i + 1) for i in range(count - 1)]
        forward.append((count - 1, 0))
        backward = [(target, source) for source, target in forward]
        low = lax.ppermute(
            lax.slice_in_dim(block, block.shape[dim] - width, None, axis=dim), axis, forward
        )
        high = lax.ppermute(lax.slice_in_dim(block, 0, width, axis=dim), axis, backward)
        block = jnp.concatenate([low, block, high], axis=dim)
    return block


def eliminate_upper(column_old, smooth):
    zero_row = jnp.zeros_like(smooth[:1])
    k_below = smooth[1:]
    k_above = jnp.concatenate([smooth[2:], zero_row], axis=0)

    def eliminate_one_level(carried, layer_data):
        offset_next, factor_next = carried
        right_side, below_k, above_k = layer_data
        pivots = 1.0 + below_k + above_k - above_k * factor_next
        offset = (right_side + above_k * offset_next) / pivots
        factor = below_k / pivots
        return ((offset, factor), (offset, factor))

    initial = (jnp.zeros_like(column_old[0]), jnp.zeros_like(column_old[0]))
    last, stacked = lax.scan(
        eliminate_one_level, initial, (column_old[2:], k_below, k_above), reverse=True, unroll=4
    )
    return (last[0], last[1], stacked[0], stacked[1])


def lower_levels(column_old, smooth, offset_two, factor_two, surface_flux):
    k_ground = smooth[0] * (1.0 + 0.5 * jnp.tanh(surface_flux))
    k_second = smooth[1]
    pivot_one = 1.0 + k_ground + k_second - k_second * factor_two
    offset_one = (column_old[1] + k_second * offset_two) / pivot_one
    factor_one = k_ground / pivot_one
    pivot_ground = 1.0 + k_ground - k_ground * factor_one
    return (
        (column_old[0] + k_ground * offset_one) / pivot_ground,
        1.0 / pivot_ground,
        offset_one,
        factor_one,
    )


def surface_solve(p_surf, q_surf, column_a, column_b):
    return (p_surf + q_surf * column_a) / (1.0 + q_surf * column_b)


def tile_sums(tile_weight, tile_coeff, tile_capacity, tile_conduct, tile_old, tile_forcing):
    fraction = tile_weight / jnp.sum(tile_weight, axis=0)
    denominator = tile_capacity + tile_coeff + tile_conduct
    source = tile_capacity * tile_old + tile_forcing
    land_a = jnp.sum(fraction * tile_coeff * source / denominator, axis=0)
    land_b = jnp.sum(fraction * tile_coeff * (tile_capacity + tile_conduct) / denominator, axis=0)
    return (land_a, land_b, denominator, source)


def substitute(surface, offset_one, factor_one, upper_offset, upper_factor):
    level_one = offset_one + factor_one * surface

    def substitute_one_level(below_value, layer_data):
        value = layer_data[0] + layer_data[1] * below_value
        return (value, value)

    unused, higher = lax.scan(
        substitute_one_level, level_one, (upper_offset, upper_factor), unroll=4
    )
    return jnp.concatenate([surface[None], level_one[None], higher], axis=0)


def build_tables(land_mask):
    columns = land_mask.shape[0]
    tile_count = columns // 128
    mask_tiles = land_mask.reshape(tile_count, 128).astype(jnp.float32)
    within = jnp.arange(128, dtype=jnp.int32)
    upper_ones = (within[:, None] <= within[None, :]).astype(jnp.float32)
    running = jnp.dot(mask_tiles, upper_ones, precision=HIGH, preferred_element_type=jnp.float32)
    tile_ids = jnp.arange(tile_count, dtype=jnp.int32)
    lower_ones = (tile_ids[None, :] < tile_ids[:, None]).astype(jnp.float32)
    offsets = jnp.dot(
        lower_ones, running[:, -1], precision=HIGH, preferred_element_type=jnp.float32
    )
    offsets_int = offsets.astype(jnp.int32)
    ranks = offsets_int[:, None] + running.astype(jnp.int32) - 1
    base_tile = offsets_int // 128
    local_place = ranks - base_tile[:, None] * 128
    window = jnp.arange(256, dtype=jnp.int32)
    selector = (
        (local_place[:, :, None] == window[None, None, :])
        & (land_mask.reshape(tile_count, 128)[:, :, None] == 1)
    ).astype(jnp.float32)
    first_half = (base_tile[None, :] == tile_ids[:, None]).astype(jnp.float32)
    second_half = (base_tile[None, :] + 1 == tile_ids[:, None]).astype(jnp.float32)
    return (selector, first_half, second_half)


def pack_rows(values, tables):
    selector, first_half, second_half = tables
    count = values.shape[0]
    tile_count = selector.shape[0]
    pieces = jnp.einsum(
        "mti,tio->mto",
        values.reshape(count, tile_count, 128),
        selector,
        precision=HIGH,
        preferred_element_type=jnp.float32,
    )
    placed = jnp.einsum(
        "jt,mtk->mjk",
        first_half,
        pieces[:, :, :128],
        precision=HIGH,
        preferred_element_type=jnp.float32,
    )
    placed = placed + jnp.einsum(
        "jt,mtk->mjk",
        second_half,
        pieces[:, :, 128:],
        precision=HIGH,
        preferred_element_type=jnp.float32,
    )
    return placed.reshape(count, tile_count * 128)


def unpack_rows(buffers, tables):
    selector, first_half, second_half = tables
    count = buffers.shape[0]
    tile_count = selector.shape[0]
    tiled = buffers.reshape(count, tile_count, 128)
    lower_part = jnp.einsum(
        "jt,mjk->mtk", first_half, tiled, precision=HIGH, preferred_element_type=jnp.float32
    )
    upper_part = jnp.einsum(
        "jt,mjk->mtk", second_half, tiled, precision=HIGH, preferred_element_type=jnp.float32
    )
    windows = jnp.concatenate([lower_part, upper_part], axis=2)
    picked = jnp.einsum(
        "mto,tio->mti", windows, selector, precision=HIGH, preferred_element_type=jnp.float32
    )
    return picked.reshape(count, tile_count * 128)


def on_device(
    column_old,
    coupling,
    sea_temp,
    land_mask,
    tile_weight,
    tile_coeff,
    tile_capacity,
    tile_conduct,
    tile_old,
    tile_forcing,
):
    columns = column_old.shape[1]
    peer_count = lax.axis_size("lon")
    slot_count = columns // peer_count
    rimmed = extended(coupling, ((("lon", "lev"), 1),), 1)
    smooth = (rimmed[:, :-2] + 2.0 * rimmed[:, 1:-1] + rimmed[:, 2:]) * 0.25
    offset_two, factor_two, upper_offset, upper_factor = eliminate_upper(column_old, smooth)
    land_a, land_b, denominator, source = tile_sums(
        tile_weight, tile_coeff, tile_capacity, tile_conduct, tile_old, tile_forcing
    )
    is_land = land_mask == 1
    tables = build_tables(land_mask)
    surface_flux = jnp.zeros_like(sea_temp)
    surface = jnp.zeros_like(sea_temp)
    offset_one = jnp.zeros_like(sea_temp)
    factor_one = jnp.zeros_like(sea_temp)
    remote_a, remote_b = (
        lax.all_to_all(land_a.reshape(columns, 1), "lon", split_axis=0, concat_axis=1, tiled=True),
        lax.all_to_all(land_b.reshape(columns, 1), "lon", split_axis=0, concat_axis=1, tiled=True),
    )
    unpacked = unpack_rows(
        jnp.stack([remote_a.reshape(columns), remote_b.reshape(columns)]), tables
    )
    column_a = jnp.where(is_land, unpacked[0], sea_temp)
    column_b = jnp.where(is_land, unpacked[1], jnp.ones_like(sea_temp))
    for repeat in range(ITERS):
        p_surf, q_surf, offset_one, factor_one = lower_levels(
            column_old, smooth, offset_two, factor_two, surface_flux
        )
        surface = surface_solve(p_surf, q_surf, column_a, column_b)
        surface_flux = column_a - column_b * surface
    packed = pack_rows(surface[None], tables)
    returned = lax.all_to_all(
        packed[0].reshape(slot_count, peer_count), "lon", split_axis=1, concat_axis=0, tiled=True
    )
    land_surface = returned.reshape(columns)
    tile_temp = (source + tile_coeff * land_surface) / denominator
    column_temp = substitute(surface, offset_one, factor_one, upper_offset, upper_factor)
    return (column_temp, tile_temp)


def solution(mesh):
    in_specs = (
        P(None, ("lon", "lev")),
        P(None, ("lon", "lev")),
        P(("lon", "lev")),
        P(("lon", "lev")),
        P(None, ("lon", "lev")),
        P(None, ("lon", "lev")),
        P(None, ("lon", "lev")),
        P(None, ("lon", "lev")),
        P(None, ("lon", "lev")),
        P(None, ("lon", "lev")),
    )
    out_specs = (P(None, ("lon", "lev")), P(None, ("lon", "lev")))
    return jax.shard_map(
        on_device, mesh=mesh, in_specs=in_specs, out_specs=out_specs, check_vma=False
    )
```

profile of v0, /device:TPU:0, one launch (start us, length us, event | category | flops | bytes accessed | tf_op | source)
XLA Modules:
  0.0 197.3 jit_solution(12235879762571774345)
XLA Ops:
  1.5 6.4 %collective-permute-start.1 = (f32[69,1]{1,0:T(8,128)S(1)}, f32[69,1]{1,0:T(8,128)S(1)}, u32[]{:S(2)}, u32[]{:S(2)}) collective-permute-start(f32[69,1]{1,0:T(8,128)S(1)} %get-tuple-element.303), channel_id=1, source_target_pairs={{1,0},{2,1},{3,2},{4,3},{5,4},{6,5},{7,6},{8,7},{9,8},{10,9},{11,1... | collective-permute-start | bytes 836 | tf_op jit(solution)/shard_map/ppermute | solution.py:21
  9.0 2.8 %fusion.28 = (f32[8192]{0:T(1024)}, f32[8192]{0:T(1024)}) fusion(f32[9,8192]{1,0:T(8,128)} %param.20, f32[9,8192]{1,0:T(8,128)} %param.21, f32[9,8192]{1,0:T(8,128)} %param.19, f32[9,8192]{1,0:T(8,128)} %param.18, f32[8192]{0:T(1024)S(1)} %reduce_sum.27, f32[9,8192]{1,0:T(8,128)} %param.23, f32[9,8192]{1,0:T(8,128)} %param.22), kind=kLoop, calls=%fused_computation.74 | loop fusion | flops 942080 | bytes 1867776 | tf_op jit(solution)/shard_map/reduce_sum | solution.py:70
  11.9 3.3 %all-to-all-start = ((f32[8,1024,1]{1,2,0:T(1,128)}), f32[8,1024,1]{1,2,0:T(1,128)S(1)}, u32[]{:S(2)}, u32[]{:S(2)}) async-start(f32[8,1024,1]{1,2,0:T(1,128)} %bitcast.19), calls=%async_computation | async-start | bytes 65536 | tf_op jit(solution)/shard_map/all_to_all | solution.py:187
  17.0 1.9 slice.243
  18.9 2.0 %reshape.118 = f32[17,4,8192]{2,1,0:T(4,128)} reshape(f32[68,8192]{1,0:T(8,128)S(1)} %slice.243) | data formatting | bytes 4456448 | tf_op jit(solution)/shard_map/reshape | solution.py:40
  20.9 4.4 %fusion.20 = f32[69,8192]{1,0:T(8,128)S(1)} fusion(f32[69,1]{1,0:T(8,128)S(1)} %collective-permute-done.1, f32[69,8192]{1,0:T(8,128)} %param.15, f32[69,1]{1,0:T(8,128)S(1)} %collective-permute-done), kind=kLoop, calls=%fused_computation.55 | loop fusion | flops 3391488 | bytes 4522536 | tf_op jit(solution)/shard_map/mul | solution.py:175
  25.5 1.6 slice.266
  27.1 1.6 concatenate.41
  28.7 3.4 %reshape.119 = f32[17,4,8192]{2,1,0:T(4,128)} reshape(f32[68,8192]{1,0:T(8,128)} %concatenate.41) | data formatting | bytes 4456448 | tf_op jit(solution)/shard_map/reshape | solution.py:40
  32.1 3.4 %reshape.120 = f32[17,4,8192]{2,1,0:T(4,128)} reshape(f32[68,8192]{1,0:T(8,128)} %slice.266) | data formatting | bytes 4456448 | tf_op jit(solution)/shard_map/reshape | solution.py:40
  35.5 1.8 broadcast.55.clone
  37.3 1.8 broadcast.55.clone.1
  39.1 84.1 %while.34 = (s32[]{:T(128)}, f32[8192]{0:T(1024)S(1)}, f32[8192]{0:T(1024)S(1)}, f32[17,4,8192]{2,1,0:T(4,128)}, f32[17,4,8192]{2,1,0:T(4,128)}, /*index=5*/f32[...) while((s32[]{:T(128)}, f32[8192]{0:T(1024)S(1)}, ...), condition=%wide.region_4.5_spmd.clone, body=%wide.region_3.4_spmd.clone.sunk | while | flops 614407 | bytes 2490620 | solution.py:40
  40.4 1.3 constant_dynamic-slice_fusion.26
  41.6 1.4 constant_dynamic-slice_fusion.27
  45.3 1.3 constant_dynamic-slice_fusion.26
  46.6 1.3 constant_dynamic-slice_fusion.27
  50.2 1.3 constant_dynamic-slice_fusion.26
  55.1 1.3 constant_dynamic-slice_fusion.26
  60.0 1.3 constant_dynamic-slice_fusion.26
  63.6 1.3 constant_dynamic-slice_fusion.25
  65.0 1.3 constant_dynamic-slice_fusion.26
  66.3 1.3 constant_dynamic-slice_fusion.27
  70.0 1.4 constant_dynamic-slice_fusion.26
  71.4 1.3 constant_dynamic-slice_fusion.27
  76.2 1.5 constant_dynamic-slice_fusion.27
  80.1 1.3 constant_dynamic-slice_fusion.26
  81.4 1.3 constant_dynamic-slice_fusion.27
  83.8 1.4 constant_dynamic-slice_fusion.25
  90.0 1.4 constant_dynamic-slice_fusion.26
  96.2 1.3 constant_dynamic-slice_fusion.27
  101.1 1.3 constant_dynamic-slice_fusion.27
  108.4 1.4 constant_dynamic-slice_fusion.25
  111.0 1.3 constant_dynamic-slice_fusion.27
  114.6 1.3 constant_dynamic-slice_fusion.26
  120.8 1.3 constant_dynamic-slice_fusion.27
  123.2 5.9 %all-to-all-start.1 = ((f32[8,1024,1]{1,2,0:T(1,128)}), f32[8,1024,1]{1,2,0:T(1,128)S(1)}, u32[]{:S(2)}, u32[]{:S(2)}) async-start(f32[8,1024,1]{1,2,0:T(1,128)} %bitcast.21), calls=%async_computation.1 | async-start | bytes 65536 | tf_op jit(solution)/shard_map/all_to_all | solution.py:188
  129.7 6.2 %all-to-all-done.1 = f32[8,1024,1]{1,2,0:T(1,128)S(1)} async-done(((f32[8,1024,1]{1,2,0:T(1,128)}), f32[8,1024,1]{1,2,0:T(1,128)S(1)}, u32[]{:S(2)}, u32[]{:S(2)}) %all-to-all-start.1) | async-done | bytes 32800 | tf_op jit(solution)/shard_map/all_to_all | solution.py:188
  136.8 5.8 %fusion.22 = f32[2,64,128]{2,0,1:T(2,128)S(1)} fusion(s32[64,128]{1,0:T(8,128)S(1)} %add_subtract_fusion.1, pred[64,128]{1,0:T(8,128)(4,1)S(1)} %fusion.62, f32[2,64,256]{2,1,0:T(8,128)S(1)} %pad_maximum_fusion.3), kind=kOutput, calls=%fused_computation.59 | convolution fusion | flops 54525952 | bytes 237568 | tf_op jit(solution)/shard_map/mto,tio->mti/dot_general | solution.py:153
  143.6 31.1 %while.33 = (s32[]{:T(128)}, f32[8192]{0:T(1024)S(1)}, f32[17,4,8192]{2,1,0:T(4,128)S(1)}, f32[17,4,8192]{2,1,0:T(4,128)}, f32[17,4,8192]{2,1,0:T(4,128)}, /*index=5*/s32[]{:T(128)}, s32[]{:T(128)}, s32[]{}, s32[]{}, s32[]{}) while((s32[]{:T(128)}, f32[8192]{0:T(1024)S(1)}, f32[17,4,8192]{2,1,0:T(4,128)S(1)}, f32[17,4,8192]{2,1,0:T(4,128)}, ...), condition=%wide.region_6.7_spmd, body=%wide.region_5.6_spmd.sunk | while | flops 163845 | bytes 1212581 | solution.py:81
  143.6 1.6 constant_dynamic-slice_fusion.24
  145.4 1.5 constant_dynamic-slice_fusion.24
  147.2 1.6 constant_dynamic-slice_fusion.24
  149.0 1.6 constant_dynamic-slice_fusion.24
  150.8 1.6 constant_dynamic-slice_fusion.24
  152.6 1.6 constant_dynamic-slice_fusion.24
  154.4 1.6 constant_dynamic-slice_fusion.24
  156.2 1.6 constant_dynamic-slice_fusion.24
  158.1 1.7 constant_dynamic-slice_fusion.24
  159.9 1.6 constant_dynamic-slice_fusion.24
  161.8 1.8 constant_dynamic-slice_fusion.24
  163.7 1.6 constant_dynamic-slice_fusion.24
  165.6 1.7 constant_dynamic-slice_fusion.24
  167.5 1.6 constant_dynamic-slice_fusion.24
  169.3 1.6 constant_dynamic-slice_fusion.24
  171.1 1.5 constant_dynamic-slice_fusion.24
  172.8 1.6 constant_dynamic-slice_fusion.24
  174.6 1.4 copy-done
  176.0 2.6 %reshape.121 = f32[68,8192]{1,0:T(8,128)S(1)} reshape(f32[17,4,8192]{2,1,0:T(4,128)} %copy-done) | data formatting | bytes 4456448 | tf_op jit(solution)/shard_map/reshape | solution.py:81
  178.6 4.8 %fusion.11 = f32[64,1,256]{2,1,0:T(1,128)S(1)} fusion(f32[64,128,1]{1,2,0:T(1,128)S(1)} %bitcast.228, s32[64,128]{1,0:T(8,128)S(1)} %add_subtract_fusion.1, pred[64,128]{1,0:T(8,128)(4,1)S(1)} %fusion.62), kind=kOutput, calls=%fused_computation.47 | convolution fusion | flops 29360128 | bytes 139264 | tf_op jit(solution)/shard_map/mti,tio->mto/dot_general | solution.py:117
  185.0 3.3 %all-to-all-start.2 = ((f32[1024,8,1]{0,2,1:T(1,128)}), f32[1024,8,1]{0,2,1:T(1,128)S(1)}, u32[]{:S(2)}, u32[]{:S(2)}) async-start(f32[1024,8,1]{0,2,1:T(1,128)} %copy.20), calls=%async_computation.2 | async-start | bytes 65536 | tf_op jit(solution)/shard_map/all_to_all | solution.py:202
  188.4 1.7 pad_maximum_fusion.2
  190.1 4.9 %all-to-all-done.2 = f32[1024,8,1]{0,2,1:T(1,128)S(1)} async-done(((f32[1024,8,1]{0,2,1:T(1,128)}), f32[1024,8,1]{0,2,1:T(1,128)S(1)}, u32[]{:S(2)}, u32[]{:S(2)}) %all-to-all-start.2) | async-done | bytes 32800 | tf_op jit(solution)/shard_map/all_to_all | solution.py:202
  195.0 2.3 %add_divide_fusion.3 = f32[9,8192]{1,0:T(8,128)} fusion(f32[9,8192]{1,0:T(8,128)} %param.19, f32[8192]{0:T(1024)S(1)} %bitcast.230, f32[9,8192]{1,0:T(8,128)S(1)} %copy-done.2, f32[9,8192]{1,0:T(8,128)S(1)} %copy-done.1, f32[9,8192]{1,0:T(8,128)} %param.23, f32[9,8192]{1,0:T(8,128)} %param.22), kind=kLoop, calls=%fused_computation.67 | loop fusion | flops 516096 | bytes 1802240 | tf_op jit(solution)/shard_map/div | solution.py:206
  (175 shorter events, 64.5 us)
Async XLA Ops:
  0.6 14.6 %copy-start.3 = (s32[8192]{0:T(1024)S(1)}, s32[8192]{0:T(1024)}, u32[]{:S(2)}) copy-start(s32[8192]{0:T(1024)} %param.17) | copy-start | bytes 98308
  1.5 19.4 %collective-permute-start.1 = (f32[69,1]{1,0:T(8,128)S(1)}, f32[69,1]{1,0:T(8,128)S(1)}, u32[]{:S(2)}, u32[]{:S(2)}) collective-permute-start(f32[69,1]{1,0:T(8,128)S(1)} %get-tuple-element.303), channel_id=1, source_target_pairs={{1,0},{2,1},{3,2},{4,3},{5,4},{6,5},{7,6},{8,7},{9,8},{10,9},{11,1... | collective-permute-start | bytes 836 | tf_op jit(solution)/shard_map/ppermute | solution.py:21
  7.9 13.0 %collective-permute-start = (f32[69,1]{1,0:T(8,128)S(1)}, f32[69,1]{1,0:T(8,128)S(1)}, u32[]{:S(2)}, u32[]{:S(2)}) collective-permute-start(f32[69,1]{1,0:T(8,128)S(1)} %get-tuple-element.302), channel_id=1, source_target_pairs={{0,1},{1,2},{2,3},{3,4},{4,5},{5,6},{6,7},{7,8},{8,9},{9,10},{10,1... | collective-permute-start | bytes 836 | tf_op jit(solution)/shard_map/ppermute | solution.py:18
  11.9 111.4 %all-to-all-start = ((f32[8,1024,1]{1,2,0:T(1,128)}), f32[8,1024,1]{1,2,0:T(1,128)S(1)}, u32[]{:S(2)}, u32[]{:S(2)}) async-start(f32[8,1024,1]{1,2,0:T(1,128)} %bitcast.19), calls=%async_computation | async-start | bytes 65536 | tf_op jit(solution)/shard_map/all_to_all | solution.py:187
  123.2 12.6 %all-to-all-start.1 = ((f32[8,1024,1]{1,2,0:T(1,128)}), f32[8,1024,1]{1,2,0:T(1,128)S(1)}, u32[]{:S(2)}, u32[]{:S(2)}) async-start(f32[8,1024,1]{1,2,0:T(1,128)} %bitcast.21), calls=%async_computation.1 | async-start | bytes 65536 | tf_op jit(solution)/shard_map/all_to_all | solution.py:188
  136.8 5.9 %copy-start.4 = (f32[8192]{0:T(1024)S(1)}, f32[8192]{0:T(1024)}, u32[]{:S(2)}) copy-start(f32[8192]{0:T(1024)} %param.16) | copy-start | bytes 98308
  174.6 1.4 copy-start
  185.0 10.0 %all-to-all-start.2 = ((f32[1024,8,1]{0,2,1:T(1,128)}), f32[1024,8,1]{0,2,1:T(1,128)S(1)}, u32[]{:S(2)}, u32[]{:S(2)}) async-start(f32[1024,8,1]{0,2,1:T(1,128)} %copy.20), calls=%async_computation.2 | async-start | bytes 65536 | tf_op jit(solution)/shard_map/all_to_all | solution.py:202
  188.4 6.6 %copy-start.1 = (f32[9,8192]{1,0:T(8,128)S(1)}, f32[9,8192]{1,0:T(8,128)}, u32[]{:S(2)}) copy-start(f32[9,8192]{1,0:T(8,128)} %param.20) | copy-start | bytes 884740
  188.4 6.6 %copy-start.2 = (f32[9,8192]{1,0:T(8,128)S(1)}, f32[9,8192]{1,0:T(8,128)}, u32[]{:S(2)}) copy-start(f32[9,8192]{1,0:T(8,128)} %param.21) | copy-start | bytes 884740
where the time goes:
time: 200 us; the launch traced here: 197 us
  local copies, waits for them, and re-layouts  119 us (60%)
  other arithmetic  34.1 us (17%)
  starting transfers between devices  19 us (10%)
  matrix products  11.9 us (6%)
  waiting for transfers between devices  11.1 us (6%)
    slice x51, local copies, waits for them, and re-layouts, eliminate_upper(): lax.scan(eliminate_one_level, initial, (column_old[2:], k_below, k_above)...  65.4 us
    slice x17, local copies, waits for them, and re-layouts, substitute(): lax.scan(substitute_one_level, level_one, (upper_offset, upper_factor), u...  27.6 us
    dynamic_update_slice x34, other arithmetic, eliminate_upper(): lax.scan(eliminate_one_level, initial, (column_old[2:], k_below, k_above)...  18.8 us
    reshape x3, local copies, waits for them, and re-layouts, eliminate_upper(): lax.scan(eliminate_one_level, initial, (column_old[2:], k_below, k_above)...  8.82 us
    ppermute x1, starting transfers between devices, extended(): lax.ppermute(lax.slice_in_dim(block, 0, width, axis=dim), axis, backward)  6.4 us
    all_to_all x1, waiting for transfers between devices, on_device(): lax.all_to_all(land_b.reshape(columns, 1), 'lon', split_axis=0, concat_ax...  6.21 us
    all_to_all x1, starting transfers between devices, on_device(): lax.all_to_all(land_b.reshape(columns, 1), 'lon', split_axis=0, concat_ax...  5.94 us
    dot_general x1, matrix products, unpack_rows(): jnp.einsum('mto,tio->mti', windows, selector, precision=HIGH, preferred_e...  5.83 us
  transfers between devices with their start and end apart: 5, of which 2 were waited for; matrix products, arithmetic and copies ran while one was open for 58% of the time, Pallas kernels for 0%

commit v1 on v0

v1 whole, which is shorter than its diff:
```python
import functools

import jax
import jax.numpy as jnp
from jax import lax
from jax.experimental import pallas as pl
from jax.experimental.pallas import tpu as pltpu
from jax.sharding import PartitionSpec as P

ITERS = 8
LANES = 128
SUB = 8
GRANT = 16 * 1024 * 1024
HIGH = lax.Precision.HIGHEST
F32 = jnp.float32
I32 = jnp.int32
VMEM = pltpu.VMEM
DMA = pltpu.SemaphoreType.DMA


def on_chip(array):
    return pltpu.with_memory_space_constraint(array, pltpu.VMEM)


def chip_call(kernel, outs, in_spaces, out_spaces, scratch, args, cost):
    results = pl.pallas_call(
        kernel,
        out_shape=outs,
        in_specs=[pl.BlockSpec(memory_space=space) for space in in_spaces],
        out_specs=[pl.BlockSpec(memory_space=space) for space in out_spaces],
        scratch_shapes=scratch,
        cost_estimate=cost,
        compiler_params=pltpu.CompilerParams(vmem_limit_bytes=GRANT),
    )(*args)
    return [
        result if isinstance(out, jax.ShapeDtypeStruct) else on_chip(result)
        for result, out in zip(results, outs)
    ]


def lane_index(shape):
    return lax.broadcasted_iota(I32, shape, len(shape) - 1)


def row_index(shape):
    return lax.broadcasted_iota(I32, shape, len(shape) - 2)


def reciprocal(x):
    return 1.0 / x


def one_hot(condition):
    return jnp.where(condition, jnp.ones((), F32), jnp.zeros((), F32))


def dot(a, b):
    return jnp.dot(a, b, precision=HIGH, preferred_element_type=F32)


def lane_of(position, fast):
    return (position & 7) * 16 + (position >> 3) if fast else position


def position_of(lane, fast):
    return (lane & 15) * 8 + (lane >> 4) if fast else lane


def rank_row_of(row, fast):
    return (row & 7) * 8 + (row >> 3) if fast else row


def exchange(blocks):
    group = lane_index((SUB, LANES)) >> 4
    step = 1
    while step < SUB:
        high = (group & step) != 0
        done = list(blocks)
        for low in range(SUB):
            if low & step:
                continue
            a, b = blocks[low], blocks[low + step]
            done[low] = jnp.where(high, pltpu.roll(b, 16 * step, 1), a)
            done[low + step] = jnp.where(high, b, pltpu.roll(a, LANES - 16 * step, 1))
        blocks = done
        step *= 2
    return blocks


def build_tables(fast, mask, source_ref, first_ref, second_ref, place_ref, fetch_ref, spot_ref):
    rows = mask.shape[0]
    shape = (rows, LANES)
    land = mask.astype(F32)
    upper = one_hot(row_index((LANES, LANES)) <= lane_index((LANES, LANES)))
    running = dot(land, upper)
    totals = dot(land, jnp.ones((LANES, LANES), F32))
    before = one_hot(lane_index((rows, rows)) < row_index((rows, rows)))
    base = dot(before, totals).astype(I32)
    totals = totals.astype(I32)
    running = running.astype(I32)
    start = base & (LANES - 1)
    position = position_of(lane_index(shape), fast)
    ordinal = (position - start) & (LANES - 1)
    source = jnp.zeros(shape, I32)
    step = LANES // 2
    while step:
        reached = jnp.take_along_axis(running, source + (step - 1), axis=1)
        source = jnp.where(reached <= ordinal, source + step, source)
        step //= 2
    source_ref[...] = source
    valid = ordinal < totals
    first_ref[...] = one_hot(valid & (position >= start))
    second_ref[...] = one_hot(valid & (position < start))
    row_totals = lax.dot_general(
        jnp.ones((SUB, LANES), F32),
        land,
        (((1,), (1,)), ((), ())),
        precision=HIGH,
        preferred_element_type=F32,
    )
    earlier = one_hot(row_index((rows, rows)) < lane_index((rows, rows)))
    base_row = dot(row_totals, earlier).astype(I32)[:1]
    lead_row = jnp.broadcast_to(base_row >> 7, (rows, rows))
    wanted = rank_row_of(row_index((rows, rows)), fast)
    place_ref[...] = jnp.concatenate(
        [one_hot(lead_row == wanted), one_hot(lead_row + 1 == wanted)], axis=1
    )
    lead = (base >> 7)[:, :rows] if rows <= LANES else base[:, :1] >> 7
    held = rank_row_of(lane_index((rows, rows)), fast)
    fetch_ref[...] = jnp.concatenate(
        [one_hot(lead == held), one_hot(lead + 1 == held)], axis=0
    )
    spot = start + running - 1
    spot_ref[...] = lane_of(spot & (LANES - 1), fast) + (spot & LANES)


def prepare(
    fast,
    coupling,
    column_old,
    mask,
    smooth,
    old,
    source,
    first,
    second,
    place,
    fetch,
    spot,
    padded,
    sem_coupling,
    sem_old,
):
    levels, rows, lanes = smooth.shape
    blocks = rows // SUB
    inner = padded.at[:, pl.ds(SUB, rows), :]
    for t in range(rows):
        pltpu.make_async_copy(
            coupling.at[:, pl.ds(t * LANES, LANES)], padded.at[:, SUB + t, :], sem_coupling
        ).start()
    for t in range(rows):
        pltpu.make_async_copy(
            column_old.at[:, pl.ds(t * LANES, LANES)], old.at[:, t, :], sem_old
        ).start()
    blank = jnp.zeros((SUB, LANES), F32)

    def clear(level, carried):
        padded[level, pl.ds(0, SUB), :] = blank
        padded[level, pl.ds(SUB + rows, SUB), :] = blank
        return carried

    lax.fori_loop(0, levels, clear, 0)
    build_tables(fast, mask[...], source, first, second, place, fetch, spot)
    lane = lane_index((SUB, LANES))
    at_last = lane == LANES - 1
    at_first = lane == 0
    pltpu.make_async_copy(inner, inner, sem_coupling).wait()

    def smooth_level(level, carried):
        for g in range(blocks):
            here = padded[level, pl.ds(SUB + g * SUB, SUB), :]
            above = padded[level, pl.ds(SUB + g * SUB - 1, SUB), :]
            below = padded[level, pl.ds(SUB + g * SUB + 1, SUB), :]
            left = pltpu.roll(jnp.where(at_last, above, here), 1, 1)
            right = pltpu.roll(jnp.where(at_first, below, here), LANES - 1, 1)
            smooth[level, pl.ds(g * SUB, SUB), :] = (left + 2.0 * here + right) * 0.25
        return carried

    lax.fori_loop(0, levels, smooth_level, 0)
    pltpu.make_async_copy(old, old, sem_old).wait()


def eliminate(
    fast,
    parity,
    smooth,
    old,
    pair_edge,
    next_edge,
    source,
    first,
    second,
    place,
    tile_weight,
    tile_coeff,
    tile_capacity,
    tile_conduct,
    tile_old,
    tile_forcing,
    offset,
    factor,
    params,
    land,
    tile_base,
    tile_slope,
    send,
    low_edge,
    high_edge,
    weight,
    coeff,
    capacity,
    conduct,
    before,
    forcing,
    sems,
):
    levels, rows, lanes = smooth.shape
    blocks = rows // SUB
    copies = [
        pltpu.make_async_copy(source_tile, buffer, sems.at[n])
        for n, (source_tile, buffer) in enumerate(
            (
                (tile_weight, weight),
                (tile_coeff, coeff),
                (tile_capacity, capacity),
                (tile_conduct, conduct),
                (tile_old, before),
                (tile_forcing, forcing),
            )
        )
    ]
    for copy in copies:
        copy.start()
    even = parity[0] == 0
    pair, following = pair_edge[...], next_edge[...]
    low_edge[...] = pltpu.roll(jnp.where(even, following, pair), 1, 1) * 0.25
    high_edge[...] = pltpu.roll(jnp.where(even, pair, following), LANES - 1, 1) * 0.25
    row, lane = row_index((SUB, LANES)), lane_index((SUB, LANES))
    low_corner = (row == 0) & (lane == 0)
    high_corner = (row == SUB - 1) & (lane == LANES - 1)
    blank = jnp.zeros((SUB, LANES), F32)

    def smooth_at(level):
        values = [smooth[level, pl.ds(g * SUB, SUB), :] for g in range(blocks)]
        low = jnp.broadcast_to(low_edge[pl.ds(level, 1), :], (SUB, LANES))
        high = jnp.broadcast_to(high_edge[pl.ds(level, 1), :], (SUB, LANES))
        values[0] = values[0] + jnp.where(low_corner, low, blank)
        values[-1] = values[-1] + jnp.where(high_corner, high, blank)
        return values

    def step(count, carried):
        level = levels - count
        conduct_u, right_n = carried
        below = smooth_at(level - 1)
        next_u, next_n = [], []
        for g in range(blocks):
            inverse = reciprocal(conduct_u[g] + below[g])
            e = right_n[g] * inverse
            offset[level - 2, pl.ds(g * SUB, SUB), :] = e
            factor[level - 2, pl.ds(g * SUB, SUB), :] = below[g] * inverse
            next_u.append(1.0 + (below[g] * conduct_u[g]) * inverse)
            next_n.append(old[level - 1, pl.ds(g * SUB, SUB), :] + below[g] * e)
        return next_u, next_n

    top = [old[levels, pl.ds(g * SUB, SUB), :] for g in range(blocks)]
    ones = [jnp.ones((SUB, LANES), F32) for _ in range(blocks)]
    conduct_u, right_n = lax.fori_loop(0, levels - 1, step, (ones, top), unroll=2)
    ground = smooth_at(0)
    for g in range(blocks):
        here = pl.ds(g * SUB, SUB)
        params[0, here, :] = old[0, here, :]
        params[1, here, :] = right_n[g]
        params[2, here, :] = conduct_u[g]
        params[3, here, :] = ground[g]
    for copy in copies:
        copy.wait()
    tiles = weight.shape[0]

    def tile_block(g, carried):
        columns = pl.ds(pl.multiple_of(g * SUB * LANES, SUB * LANES), SUB * LANES)
        here = pl.ds(pl.multiple_of(g * SUB, SUB), SUB)
        weight_sum = land_a = land_b = blank
        for t in range(tiles):
            w, c, cap, con, was, force = (
                buffer[t, columns].reshape(SUB, LANES)
                for buffer in (weight, coeff, capacity, conduct, before, forcing)
            )
            keep = cap + con
            inverse = reciprocal(keep + c)
            src = cap * was + force
            slope = c * inverse
            tile_base[t, here, :] = src * inverse
            tile_slope[t, here, :] = slope
            share = w * slope
            weight_sum = weight_sum + w
            land_a = land_a + share * src
            land_b = land_b + share * keep
        inverse = reciprocal(weight_sum)
        land[0, here, :] = land_a * inverse
        land[1, here, :] = land_b * inverse
        return carried

    lax.fori_loop(0, blocks, tile_block, 0)
    pick, lead, rest = source[...], first[...], second[...]
    halves = []
    for n in range(4):
        moved = jnp.take_along_axis(params[n], pick, axis=1)
        halves.append(jnp.concatenate([moved * lead, moved * rest], axis=0))
    packed = dot(place[...], jnp.concatenate(halves, axis=1))
    for n in range(4):
        field = packed[:, n * LANES : (n + 1) * LANES]
        if fast:
            for k, block in enumerate(exchange([field[g * SUB : (g + 1) * SUB] for g in range(blocks)])):
                send[k, 2 + n] = block
        else:
            send[n] = field
    if fast:
        for k in range(blocks):
            for n in range(2):
                send[k, n] = land[n, pl.ds(k * SUB, SUB), :]


def finish(
    fast,
    inbox,
    slots,
    offset,
    factor,
    params,
    land,
    tile_base,
    tile_slope,
    fetch,
    spot,
    mask,
    sea,
    column_temp,
    tile_temp,
    solved,
    warm,
    column_buffer,
    tile_buffer,
    sems,
    tile_sem,
):
    upper, rows, lanes = offset.shape
    blocks = rows // SUB
    levels = upper + 2
    tiles = tile_base.shape[0]
    fields = []
    for n in range(2):
        if fast:
            fields.append(
                jnp.concatenate(exchange([inbox[k, n] for k in range(blocks)]), axis=0)
            )
        else:
            fields.append(inbox[n])
    windows = dot(fetch[...], jnp.concatenate(fields, axis=1))
    place = spot[...]
    lane, upper_half = place & (LANES - 1), place >= LANES
    is_land = mask[...] == 1
    for n, ocean in ((0, sea[...]), (1, jnp.ones((rows, LANES), F32))):
        one = windows[:rows, n * LANES : (n + 1) * LANES]
        two = windows[rows:, n * LANES : (n + 1) * LANES]
        found = jnp.where(
            upper_half,
            jnp.take_along_axis(two, lane, axis=1),
            jnp.take_along_axis(one, lane, axis=1),
        )
        solved[n, pl.ds(0, rows), :] = jnp.where(is_land, found, ocean)
        solved[n, pl.ds(rows, rows), :] = land[n]
    for n in range(4):
        solved[2 + n, pl.ds(0, rows), :] = params[n]
        for i in range(blocks):
            got = inbox[i, 2 + n] if fast else slots[n, pl.ds(i * SUB, SUB), :]
            solved[2 + n, pl.ds(rows + i * SUB, SUB), :] = got
    everything = 2 * blocks

    def iterate(repeat, flux):
        fluxes = []
        for g in range(everything):
            here = pl.ds(g * SUB, SUB)
            a, b = solved[0, here, :], solved[1, here, :]
            base, n1, w, ground = (solved[2 + n, here, :] for n in range(4))
            if g >= blocks:
                w = jnp.where(ground > 0.0, w, 1.0)
            k = ground * (1.0 + 0.5 * jnp.tanh(flux[g]))
            total = w + k
            top = (base + a) * total + k * n1
            bottom = (1.0 + b) * total + w * k
            surface = top * reciprocal(bottom)
            if g >= blocks:
                warm[pl.ds((g - blocks) * SUB, SUB), :] = jnp.where(ground > 0.0, surface, 0.0)
            else:
                column_buffer[0, here, :] = surface
                column_buffer[1, here, :] = k
            fluxes.append(a - b * surface)
        return fluxes

    zero = jnp.zeros((SUB, LANES), F32)
    lax.fori_loop(0, ITERS, iterate, [zero] * everything)
    for t in range(tiles):
        tile_buffer[t] = tile_base[t] + tile_slope[t] * warm[...]
    for t in range(rows):
        pltpu.make_async_copy(
            tile_buffer.at[:, t, :], tile_temp.at[:, pl.ds(t * LANES, LANES)], tile_sem
        ).start()
    width = 2
    for part in range(blocks // width):
        spans = [pl.ds((part * width + g) * SUB, SUB) for g in range(width)]
        values = []
        for here in spans:
            surface, k = column_buffer[0, here, :], column_buffer[1, here, :]
            n1, w = params[1, here, :], params[2, here, :]
            value = (n1 + k * surface) * reciprocal(w + k)
            column_buffer[1, here, :] = value
            values.append(value)

        def substitute(level, values):
            values = [
                offset[level, here, :] + factor[level, here, :] * value
                for here, value in zip(spans, values)
            ]
            for here, value in zip(spans, values):
                column_buffer[level + 2, here, :] = value
            return values

        lax.fori_loop(0, upper, substitute, values, unroll=4)
        for t in range(part * width * SUB, (part + 1) * width * SUB):
            pltpu.make_async_copy(
                column_buffer.at[:, t, :],
                column_temp.at[:, pl.ds(t * LANES, LANES)],
                sems.at[part],
            ).start()
    pltpu.make_async_copy(tile_buffer, tile_buffer, tile_sem).wait()
    for part in range(blocks // width):
        span = column_buffer.at[:, pl.ds(part * width * SUB, width * SUB), :]
        pltpu.make_async_copy(span, span, sems.at[part]).wait()


def on_device(
    column_old,
    coupling,
    sea_temp,
    land_mask,
    tile_weight,
    tile_coeff,
    tile_capacity,
    tile_conduct,
    tile_old,
    tile_forcing,
):
    axes = ("lon", "lev")
    couplings, columns = coupling.shape
    levels = column_old.shape[0]
    tiles = tile_weight.shape[0]
    peers = lax.axis_size("lon")
    slot_count = columns // peers
    rows = columns // LANES
    blocks = rows // SUB
    fast = peers == SUB and rows == SUB * SUB
    devices = peers * lax.axis_size("lev")
    parity = lax.rem(lax.axis_index(axes), 2)
    first_edge, last_edge = coupling[:, :LANES], coupling[:, columns - LANES :]
    even = parity == 0
    pairs = [(i, i ^ 1) for i in range(devices)]
    following = [(i, (i + 1 if i % 2 else i - 1) % devices) for i in range(devices)]
    next_edge = lax.ppermute(jnp.where(even, first_edge, last_edge), axes, following)
    pair_edge = lax.ppermute(jnp.where(even, last_edge, first_edge), axes, pairs)

    hbm, vmem, smem = pl.ANY, pltpu.VMEM, pltpu.SMEM
    full = (rows, LANES)
    mask = land_mask.reshape(full)
    table_outs = [
        VMEM(full, I32),
        VMEM(full, F32),
        VMEM(full, F32),
        VMEM((rows, 2 * rows), F32),
        VMEM((2 * rows, rows), F32),
        VMEM(full, I32),
    ]
    smooth, old, source, first, second, place, fetch, spot = chip_call(
        functools.partial(prepare, fast),
        [VMEM((couplings,) + full, F32), VMEM((levels,) + full, F32)] + table_outs,
        [hbm, hbm, vmem],
        [vmem] * 8,
        [VMEM((couplings, rows + 2 * SUB, LANES), F32), DMA, DMA],
        (coupling, column_old, mask),
        pl.CostEstimate(
            flops=8 * couplings * columns, bytes_accessed=8 * levels * columns, transcendentals=0
        ),
    )
    sent = (peers, 6, SUB, LANES) if fast else (4,) + full
    handed = VMEM if fast else jax.ShapeDtypeStruct
    offset, factor, params, land, tile_base, tile_slope, send = chip_call(
        functools.partial(eliminate, fast),
        [
            VMEM((levels - 2,) + full, F32),
            VMEM((levels - 2,) + full, F32),
            VMEM((4,) + full, F32),
            handed((2,) + full, F32),
            VMEM((tiles,) + full, F32),
            VMEM((tiles,) + full, F32),
            handed(sent, F32),
        ],
        [smem] + [vmem] * 8 + [hbm] * 6,
        [vmem] * 7,
        [VMEM((couplings, LANES), F32)] * 2 + [VMEM((tiles, columns), F32)] * 6 + [DMA((6,))],
        (
            parity.reshape(1),
            smooth,
            old,
            pair_edge,
            next_edge,
            source,
            first,
            second,
            place,
            tile_weight,
            tile_coeff,
            tile_capacity,
            tile_conduct,
            tile_old,
            tile_forcing,
        ),
        pl.CostEstimate(
            flops=20 * levels * columns, bytes_accessed=24 * tiles * columns, transcendentals=0
        ),
    )
    if fast:
        inbox = lax.all_to_all(send, "lon", split_axis=0, concat_axis=0, tiled=True)
        slots = inbox
    else:
        ranked = send.reshape(4, slot_count, peers).transpose(2, 0, 1)
        own = land.reshape(2, peers, slot_count).transpose(1, 0, 2)
        got = lax.all_to_all(
            jnp.concatenate([own, ranked], axis=1), "lon", split_axis=0, concat_axis=0, tiled=True
        )
        inbox = got[:, :2].transpose(1, 2, 0).reshape((2,) + full)
        slots = got[:, 2:].transpose(1, 0, 2).reshape((4,) + full)
    width = 2
    column_temp, tile_temp = chip_call(
        functools.partial(finish, fast),
        [
            jax.ShapeDtypeStruct(column_old.shape, F32),
            jax.ShapeDtypeStruct(tile_old.shape, F32),
        ],
        [vmem] * 12,
        [hbm, hbm],
        [
            VMEM((6, 2 * rows, LANES), F32),
            VMEM(full, F32),
            VMEM((levels,) + full, F32),
            VMEM((tiles,) + full, F32),
            DMA((blocks // width,)),
            DMA,
        ],
        (
            inbox,
            slots,
            offset,
            factor,
            params,
            land,
            tile_base,
            tile_slope,
            fetch,
            spot,
            mask,
            sea_temp.reshape(full),
        ),
        pl.CostEstimate(
            flops=4 * levels * columns, bytes_accessed=4 * levels * columns, transcendentals=0
        ),
    )
    return column_temp, tile_temp


def solution(mesh):
    wide, flat = P(None, ("lon", "lev")), P(("lon", "lev"))
    in_specs = (wide, wide, flat, flat) + (wide,) * 6
    return jax.shard_map(
        on_device, mesh=mesh, in_specs=in_specs, out_specs=(wide, wide), check_vma=False
    )
```

time: 200 us -> 41.2 us (0.21); the launches traced: 197 us -> 40.8 us
  local copies, waits for them, and re-layouts: 119 us -> 4.13 us
  other arithmetic: 34.1 us -> 0.8 us
  Pallas kernels: 0 us -> 17.4 us
  starting transfers between devices: 19 us -> 6.4 us
  matrix products: 11.9 us -> 0 us
  blocking collectives: 0 us -> 11.3 us
  waiting for transfers between devices: 11.1 us -> 0.01 us
    slice x76 -> x0, local copies, waits for them, and re-layouts: 98.9 us -> none  [the longest x51 65.4 us: eliminate_upper(): lax.scan(eliminate_one_level, initial, (column_old[2:], k_below, k_above)...]
    dynamic_update_slice x34 -> x0, other arithmetic: 18.8 us -> none  [eliminate_upper(): lax.scan(eliminate_one_level, initial, (column_old[2:], k_below, k_above)...]
    pallas_call x0 -> x3, Pallas kernels: none -> 17.4 us  [chip_call(): pl.pallas_call(kernel, out_shape=outs, in_specs=[pl.BlockSpec(memory_spac...]
    all_to_all x3 -> x0, starting transfers between devices: 12.6 us -> none  [the longest x1 5.94 us: on_device(): lax.all_to_all(land_b.reshape(columns, 1), 'lon', split_axis=0, concat_ax...]
    dot_general x8 -> x0, matrix products: 11.9 us -> none  [the longest x1 5.83 us: unpack_rows(): jnp.einsum('mto,tio->mti', windows, selector, precision=HIGH, preferred_e...]
    reshape x4 -> x0, local copies, waits for them, and re-layouts: 11.4 us -> none  [the longest x3 8.82 us: eliminate_upper(): lax.scan(eliminate_one_level, initial, (column_old[2:], k_below, k_above)...]
    all_to_all x0 -> x1, blocking collectives: none -> 11.3 us  [on_device(): inbox = lax.all_to_all(send, 'lon', split_axis=0, concat_axis=0, tiled=True)]
    all_to_all x3 -> x0, waiting for transfers between devices: 11.1 us -> none  [the longest x1 6.21 us: on_device(): lax.all_to_all(land_b.reshape(columns, 1), 'lon', split_axis=0, concat_ax...]
  transfers between devices with their start and end apart: 5 -> 2, of which waited for: 2 -> 0; matrix products, arithmetic and copies ran while one was open for 58% -> 0% of each run, Pallas kernels for 0% -> 28%
where the time goes in v1:
time: 41.2 us; the launch traced here: 40.8 us
  Pallas kernels  17.4 us (42%)
  blocking collectives  11.3 us (27%)
  starting transfers between devices  6.4 us (16%)
  local copies, waits for them, and re-layouts  4.13 us (10%)
  other arithmetic  0.8 us (2%)
  between operations  0.76 us (2%)
    pallas_call x3, Pallas kernels, chip_call(): pl.pallas_call(kernel, out_shape=outs, in_specs=[pl.BlockSpec(memory_spac...  17.4 us
    all_to_all x1, blocking collectives, on_device(): inbox = lax.all_to_all(send, 'lon', split_axis=0, concat_axis=0, tiled=True)  11.3 us
    ppermute x1, starting transfers between devices, on_device(): lax.ppermute(jnp.where(even, first_edge, last_edge), axes, following)  6.4 us
    unnamed x22, local copies, waits for them, and re-layouts  4.13 us
  transfers between devices with their start and end apart: 2, of which 0 were waited for; matrix products, arithmetic and copies ran while one was open for 0% of the time, Pallas kernels for 28%

profile of v1, /device:TPU:0, one launch (start us, length us, event | category | flops | bytes accessed | tf_op | source)
XLA Modules:
  0.0 40.8 jit_solution(14786062937394500129)
XLA Ops:
  0.6 0.8 %slice_select_fusion = (f32[69,128]{1,0:T(8,128)S(1)}, f32[69,128]{1,0:T(8,128)S(1)}) fusion(f32[69,8192]{1,0:T(8,128)} %coupling.1, pred[]{:T(512)S(6)} %eq.3), kind=kLoop, calls=%fused_computation | loop fusion | flops 17664 | bytes 141313 | tf_op jit(solution)/shard_map/jit(_where)/select_n | solution.py:478
  1.4 6.4 %collective-permute-start.1 = (f32[69,128]{1,0:T(8,128)S(1)}, f32[69,128]{1,0:T(8,128)S(1)}, u32[]{:S(2)}, u32[]{:S(2)}) collective-permute-start(f32[69,128]{1,0:T(8,128)S(1)} %get-tuple-element.32), channel_id=1, source_target_pairs={{0,31},{1,2},{2,1},{3,4},{4,3},{5,6},{6,5},{7,8},{8,7},{9,10},{10,... | collective-permute-start | bytes 105992 | tf_op jit(solution)/shard_map/ppermute | solution.py:478
  7.8 0.0 collective-permute-start
  7.8 0.0 copy-start
  7.8 1.7 %copy-done = f32[69,8192]{1,0:T(8,128)S(1)} copy-done((f32[69,8192]{1,0:T(8,128)S(1)}, f32[69,8192]{1,0:T(8,128)}, u32[]{:S(2)}) %copy-start) | copy-done | bytes 2261016
  9.5 0.0 copy-start.1
  9.5 1.7 %copy-done.1 = f32[70,8192]{1,0:T(8,128)S(1)} copy-done((f32[70,8192]{1,0:T(8,128)S(1)}, f32[70,8192]{1,0:T(8,128)}, u32[]{:S(2)}) %copy-start.1) | copy-done | bytes 2293784
  11.2 0.0 copy-start.8
  11.2 0.8 %copy-done.8 = s32[8192]{0:T(1024)S(1)} copy-done((s32[8192]{0:T(1024)S(1)}, s32[8192]{0:T(1024)}, u32[]{:S(2)}) %copy-start.8) | copy-done | bytes 32792
  11.9 0.0 copy-start.2
  11.9 0.0 copy-start.3
  11.9 0.0 copy-start.4
  11.9 0.0 copy-start.5
  11.9 0.0 copy-start.6
  12.0 0.0 copy-start.7
  12.0 11.5 %shard_map.113 = (f32[69,64,128]{2,1,0:T(8,128)S(1)}, f32[70,64,128]{2,1,0:T(8,128)S(1)}, s32[64,128]{1,0:T(8,128)S(1)}, f32[64,128]{1,0:T(8,128)S(1)}, f32[64,1...) custom-call(f32[69,8192]{1,0:T(8,128)S(1)} %copy-done, ...), custom_call_target="tpu_custom_call" | custom-call | flops 4521984 | bytes 4587520 | tf_op jit(solution)/shard_map/pallas_call | solution.py:26
  23.4 0.0 collective-permute-done.1.next_edge
  23.4 0.0 collective-permute-done.pair_edge
  23.5 0.0 copy-done.2
  23.5 0.0 copy-done.3
  23.5 0.0 copy-done.4
  23.5 0.0 copy-done.5
  23.5 0.0 copy-done.6
  23.5 0.0 copy-done.7
  23.5 0.0 copy-start.9
  23.5 0.0 copy-start.10
  23.5 2.7 %shard_map.114 = (f32[68,64,128]{2,1,0:T(8,128)S(1)}, f32[68,64,128]{2,1,0:T(8,128)S(1)}, f32[4,64,128]{2,1,0:T(8,128)S(1)}, f32[2,64,128]{2,1,0:T(8,128)S(1)}, ...) custom-call(s32[1]{0:T(128)} %bitcast.parity, ...), custom_call_target="tpu_custom_call" | custom-call | flops 11468800 | bytes 1769472 | tf_op jit(solution)/shard_map/pallas_call | solution.py:26
  26.2 11.3 %all_to_all.5.inbox.slots = f32[8,6,8,128]{3,2,1,0:T(8,128)S(1)} all-to-all(f32[8,6,8,128]{3,2,1,0:T(8,128)S(1)} %get-tuple-element.23), channel_id=1, replica_groups=mesh['lon'=8,'lev'=4] {'lon'}, dimensions={0} | all-to-all | bytes 393216 | tf_op jit(solution)/shard_map/all_to_all | solution.py:541
  37.5 0.0 copy-done.9
  37.5 0.0 copy-done.10
  37.5 3.3 %shard_map.115 = (f32[70,8192]{1,0:T(8,128)}, f32[9,8192]{1,0:T(8,128)}) custom-call(f32[8,6,8,128]{3,2,1,0:T(8,128)S(1)} %all_to_all.5.inbox.slots, f32[8,6,8,128]{3,2,1,0:T(8,128)S(1)} %all_to_all.5.inbox.slots, f32[68,64,128]{2,1,0:T(8,128)S(1)} %get-tuple-element.24.offset, f32[68,64,128]{2,1,0:T(8,128)S(1)} %get-tuple-element.25.factor, ...), custom_call_target="tpu_custom_call" | custom-call | flops 2293760 | bytes 2293760 | tf_op jit(solution)/shard_map/pallas_call | solution.py:26
Async XLA Ops:
  1.4 22.0 %collective-permute-start.1 = (f32[69,128]{1,0:T(8,128)S(1)}, f32[69,128]{1,0:T(8,128)S(1)}, u32[]{:S(2)}, u32[]{:S(2)}) collective-permute-start(f32[69,128]{1,0:T(8,128)S(1)} %get-tuple-element.32), channel_id=1, source_target_pairs={{0,31},{1,2},{2,1},{3,4},{4,3},{5,6},{6,5},{7,8},{8,7},{9,10},{10,... | collective-permute-start | bytes 105992 | tf_op jit(solution)/shard_map/ppermute | solution.py:478
  7.8 15.6 %collective-permute-start = (f32[69,128]{1,0:T(8,128)S(1)}, f32[69,128]{1,0:T(8,128)S(1)}, u32[]{:S(2)}, u32[]{:S(2)}) collective-permute-start(f32[69,128]{1,0:T(8,128)S(1)} %get-tuple-element.33), channel_id=1, source_target_pairs={{0,1},{1,0},{2,3},{3,2},{4,5},{5,4},{6,7},{7,6},{8,9},{9,8},{10,11... | collective-permute-start | bytes 105992 | tf_op jit(solution)/shard_map/ppermute | solution.py:479
  7.8 1.7 %copy-start = (f32[69,8192]{1,0:T(8,128)S(1)}, f32[69,8192]{1,0:T(8,128)}, u32[]{:S(2)}) copy-start(f32[69,8192]{1,0:T(8,128)} %coupling.1) | copy-start | bytes 6782980
  9.5 1.7 %copy-start.1 = (f32[70,8192]{1,0:T(8,128)S(1)}, f32[70,8192]{1,0:T(8,128)}, u32[]{:S(2)}) copy-start(f32[70,8192]{1,0:T(8,128)} %column_old.1) | copy-start | bytes 6881284
  11.2 0.8 %copy-start.8 = (s32[8192]{0:T(1024)S(1)}, s32[8192]{0:T(1024)}, u32[]{:S(2)}) copy-start(s32[8192]{0:T(1024)} %param.13) | copy-start | bytes 98308
  11.9 11.5 %copy-start.2 = (f32[9,8192]{1,0:T(8,128)S(1)}, f32[9,8192]{1,0:T(8,128)}, u32[]{:S(2)}) copy-start(f32[9,8192]{1,0:T(8,128)} %tile_weight.1) | copy-start | bytes 884740
  11.9 11.5 %copy-start.3 = (f32[9,8192]{1,0:T(8,128)S(1)}, f32[9,8192]{1,0:T(8,128)}, u32[]{:S(2)}) copy-start(f32[9,8192]{1,0:T(8,128)} %tile_coeff.1) | copy-start | bytes 884740
  11.9 11.6 %copy-start.4 = (f32[9,8192]{1,0:T(8,128)S(1)}, f32[9,8192]{1,0:T(8,128)}, u32[]{:S(2)}) copy-start(f32[9,8192]{1,0:T(8,128)} %tile_capacity.1) | copy-start | bytes 884740
  11.9 11.6 %copy-start.5 = (f32[9,8192]{1,0:T(8,128)S(1)}, f32[9,8192]{1,0:T(8,128)}, u32[]{:S(2)}) copy-start(f32[9,8192]{1,0:T(8,128)} %tile_conduct.1) | copy-start | bytes 884740
  11.9 11.6 %copy-start.6 = (f32[9,8192]{1,0:T(8,128)S(1)}, f32[9,8192]{1,0:T(8,128)}, u32[]{:S(2)}) copy-start(f32[9,8192]{1,0:T(8,128)} %tile_old.1) | copy-start | bytes 884740
  12.0 11.6 %copy-start.7 = (f32[9,8192]{1,0:T(8,128)S(1)}, f32[9,8192]{1,0:T(8,128)}, u32[]{:S(2)}) copy-start(f32[9,8192]{1,0:T(8,128)} %tile_forcing.1) | copy-start | bytes 884740
  23.5 14.0 %copy-start.9 = (s32[8192]{0:T(1024)S(1)}, s32[8192]{0:T(1024)}, u32[]{:S(2)}) copy-start(s32[8192]{0:T(1024)} %param.13) | copy-start | bytes 98308
  23.5 14.0 %copy-start.10 = (f32[8192]{0:T(1024)S(1)}, f32[8192]{0:T(1024)}, u32[]{:S(2)}) copy-start(f32[8192]{0:T(1024)} %param.12) | copy-start | bytes 98308

commit v2 on v1

--- a/solution.py
+++ b/solution.py
@@ -11,6 +11,7 @@
 LANES = 128
 SUB = 8
 GRANT = 16 * 1024 * 1024
+WIDE_GRANT = 55 * 1024 * 1024
 HIGH = lax.Precision.HIGHEST
 F32 = jnp.float32
 I32 = jnp.int32
@@ -22,7 +23,7 @@
     return pltpu.with_memory_space_constraint(array, pltpu.VMEM)
 
 
-def chip_call(kernel, outs, in_spaces, out_spaces, scratch, args, cost):
+def chip_call(kernel, outs, in_spaces, out_spaces, scratch, args, cost, grant=GRANT):
     results = pl.pallas_call(
         kernel,
         out_shape=outs,
@@ -30,7 +31,7 @@
         out_specs=[pl.BlockSpec(memory_space=space) for space in out_spaces],
         scratch_shapes=scratch,
         cost_estimate=cost,
-        compiler_params=pltpu.CompilerParams(vmem_limit_bytes=GRANT),
+        compiler_params=pltpu.CompilerParams(vmem_limit_bytes=grant),
     )(*args)
     return [
         result if isinstance(out, jax.ShapeDtypeStruct) else on_chip(result)
@@ -169,7 +170,7 @@
         padded[level, pl.ds(SUB + rows, SUB), :] = blank
         return carried
 
-    lax.fori_loop(0, levels, clear, 0)
+    lax.fori_loop(0, levels, clear, 0, unroll=3)
     build_tables(fast, mask[...], source, first, second, place, fetch, spot)
     lane = lane_index((SUB, LANES))
     at_last = lane == LANES - 1
@@ -186,7 +187,7 @@
             smooth[level, pl.ds(g * SUB, SUB), :] = (left + 2.0 * here + right) * 0.25
         return carried
 
-    lax.fori_loop(0, levels, smooth_level, 0)
+    lax.fori_loop(0, levels, smooth_level, 0, unroll=levels // 3)
     pltpu.make_async_copy(old, old, sem_old).wait()
 
 
@@ -499,6 +500,7 @@
         pl.CostEstimate(
             flops=8 * couplings * columns, bytes_accessed=8 * levels * columns, transcendentals=0
         ),
+        WIDE_GRANT,
     )
     sent = (peers, 6, SUB, LANES) if fast else (4,) + full
     handed = VMEM if fast else jax.ShapeDtypeStruct

time: 41.2 us -> 29.6 us (0.72)
  Pallas kernels: 17.4 us -> 10.1 us
  local copies, waits for them, and re-layouts: 4.13 us -> 0.04 us
    pallas_call x3, Pallas kernels: 17.4 us -> 10.1 us  [chip_call(): pl.pallas_call(kernel, out_shape=outs, in_specs=[pl.BlockSpec(memory_spac...]
    unnamed x22 -> x16, local copies, waits for them, and re-layouts: 4.13 us -> 0.04 us
  transfers between devices with their start and end apart: 2 -> 2, of which waited for: 0 -> 0; matrix products, arithmetic and copies ran while one was open for 0% -> 0% of each run, Pallas kernels for 28% -> 14%
where the time goes in v2:
time: 29.6 us; the launch traced here: 29.3 us
  blocking collectives  11.3 us (38%)
  Pallas kernels  10.1 us (34%)
  starting transfers between devices  6.4 us (22%)
  other arithmetic  0.8 us (3%)
  between operations  0.77 us (3%)
    all_to_all x1, blocking collectives, on_device(): inbox = lax.all_to_all(send, 'lon', split_axis=0, concat_axis=0, tiled=True)  11.3 us
    pallas_call x3, Pallas kernels, chip_call(): pl.pallas_call(kernel, out_shape=outs, in_specs=[pl.BlockSpec(memory_spac...  10.1 us
    ppermute x1, starting transfers between devices, on_device(): lax.ppermute(jnp.where(even, first_edge, last_edge), axes, following)  6.4 us
    select_n x1, other arithmetic, on_device(): jnp.where(even, first_edge, last_edge)  0.8 us
  transfers between devices with their start and end apart: 2, of which 0 were waited for; matrix products, arithmetic and copies ran while one was open for 0% of the time, Pallas kernels for 14%

profile of v2, /device:TPU:0, one launch (start us, length us, event | category | flops | bytes accessed | tf_op | source)
XLA Modules:
  0.0 29.3 jit_solution(5871534081370173318)
XLA Ops:
  0.6 0.8 %slice_select_fusion = (f32[69,128]{1,0:T(8,128)S(1)}, f32[69,128]{1,0:T(8,128)S(1)}) fusion(f32[69,8192]{1,0:T(8,128)} %coupling.1, pred[]{:T(512)S(6)} %eq.3), kind=kLoop, calls=%fused_computation | loop fusion | flops 17664 | bytes 141313 | tf_op jit(solution)/shard_map/jit(_where)/select_n | solution.py:479
  1.4 6.4 %collective-permute-start.1 = (f32[69,128]{1,0:T(8,128)S(1)}, f32[69,128]{1,0:T(8,128)S(1)}, u32[]{:S(2)}, u32[]{:S(2)}) collective-permute-start(f32[69,128]{1,0:T(8,128)S(1)} %get-tuple-element.32), channel_id=1, source_target_pairs={{0,31},{1,2},{2,1},{3,4},{4,3},{5,6},{6,5},{7,8},{8,7},{9,10},{10,... | collective-permute-start | bytes 105992 | tf_op jit(solution)/shard_map/ppermute | solution.py:479
  7.8 0.0 collective-permute-start
  7.8 0.0 copy-start
  7.8 0.0 copy-start.1
  7.8 0.0 copy-start.2
  7.8 0.0 copy-start.3
  7.9 0.0 copy-start.4
  7.9 0.0 copy-start.5
  7.9 4.1 %shard_map.113 = (f32[69,64,128]{2,1,0:T(8,128)S(1)}, f32[70,64,128]{2,1,0:T(8,128)S(1)}, s32[64,128]{1,0:T(8,128)S(1)}, f32[64,128]{1,0:T(8,128)S(1)}, f32[64,1...) custom-call(f32[69,8192]{1,0:T(8,128)} %coupling.1, ...), custom_call_target="tpu_custom_call" | custom-call | flops 4521984 | bytes 4587520 | tf_op jit(solution)/shard_map/pallas_call | solution.py:27
  12.0 0.0 collective-permute-done.1.next_edge
  12.0 0.0 collective-permute-done.pair_edge
  12.0 0.0 copy-done
  12.1 0.0 copy-done.1
  12.1 0.0 copy-done.2
  12.1 0.0 copy-done.3
  12.1 0.0 copy-done.4
  12.1 0.0 copy-done.5
  12.1 0.0 copy-start.6
  12.1 0.0 copy-start.7
  12.1 2.7 %shard_map.114 = (f32[68,64,128]{2,1,0:T(8,128)S(1)}, f32[68,64,128]{2,1,0:T(8,128)S(1)}, f32[4,64,128]{2,1,0:T(8,128)S(1)}, f32[2,64,128]{2,1,0:T(8,128)S(1)}, ...) custom-call(s32[1]{0:T(128)} %bitcast.parity, ...), custom_call_target="tpu_custom_call" | custom-call | flops 11468800 | bytes 1769472 | tf_op jit(solution)/shard_map/pallas_call | solution.py:27
  14.8 11.3 %all_to_all.5.inbox.slots = f32[8,6,8,128]{3,2,1,0:T(8,128)S(1)} all-to-all(f32[8,6,8,128]{3,2,1,0:T(8,128)S(1)} %get-tuple-element.23), channel_id=1, replica_groups=mesh['lon'=8,'lev'=4] {'lon'}, dimensions={0} | all-to-all | bytes 393216 | tf_op jit(solution)/shard_map/all_to_all | solution.py:543
  26.1 0.0 copy-done.6
  26.1 0.0 copy-done.7
  26.1 3.3 %shard_map.115 = (f32[70,8192]{1,0:T(8,128)}, f32[9,8192]{1,0:T(8,128)}) custom-call(f32[8,6,8,128]{3,2,1,0:T(8,128)S(1)} %all_to_all.5.inbox.slots, f32[8,6,8,128]{3,2,1,0:T(8,128)S(1)} %all_to_all.5.inbox.slots, f32[68,64,128]{2,1,0:T(8,128)S(1)} %get-tuple-element.24.offset, f32[68,64,128]{2,1,0:T(8,128)S(1)} %get-tuple-element.25.factor, ...), custom_call_target="tpu_custom_call" | custom-call | flops 2293760 | bytes 2293760 | tf_op jit(solution)/shard_map/pallas_call | solution.py:27
Async XLA Ops:
  1.4 10.6 %collective-permute-start.1 = (f32[69,128]{1,0:T(8,128)S(1)}, f32[69,128]{1,0:T(8,128)S(1)}, u32[]{:S(2)}, u32[]{:S(2)}) collective-permute-start(f32[69,128]{1,0:T(8,128)S(1)} %get-tuple-element.32), channel_id=1, source_target_pairs={{0,31},{1,2},{2,1},{3,4},{4,3},{5,6},{6,5},{7,8},{8,7},{9,10},{10,... | collective-permute-start | bytes 105992 | tf_op jit(solution)/shard_map/ppermute | solution.py:479
  7.8 4.2 %collective-permute-start = (f32[69,128]{1,0:T(8,128)S(1)}, f32[69,128]{1,0:T(8,128)S(1)}, u32[]{:S(2)}, u32[]{:S(2)}) collective-permute-start(f32[69,128]{1,0:T(8,128)S(1)} %get-tuple-element.33), channel_id=1, source_target_pairs={{0,1},{1,0},{2,3},{3,2},{4,5},{5,4},{6,7},{7,6},{8,9},{9,8},{10,11... | collective-permute-start | bytes 105992 | tf_op jit(solution)/shard_map/ppermute | solution.py:480
  7.8 4.2 %copy-start = (f32[9,8192]{1,0:T(8,128)S(1)}, f32[9,8192]{1,0:T(8,128)}, u32[]{:S(2)}) copy-start(f32[9,8192]{1,0:T(8,128)} %tile_weight.1) | copy-start | bytes 884740
  7.8 4.2 %copy-start.1 = (f32[9,8192]{1,0:T(8,128)S(1)}, f32[9,8192]{1,0:T(8,128)}, u32[]{:S(2)}) copy-start(f32[9,8192]{1,0:T(8,128)} %tile_coeff.1) | copy-start | bytes 884740
  7.8 4.2 %copy-start.2 = (f32[9,8192]{1,0:T(8,128)S(1)}, f32[9,8192]{1,0:T(8,128)}, u32[]{:S(2)}) copy-start(f32[9,8192]{1,0:T(8,128)} %tile_capacity.1) | copy-start | bytes 884740
  7.8 4.2 %copy-start.3 = (f32[9,8192]{1,0:T(8,128)S(1)}, f32[9,8192]{1,0:T(8,128)}, u32[]{:S(2)}) copy-start(f32[9,8192]{1,0:T(8,128)} %tile_conduct.1) | copy-start | bytes 884740
  7.9 4.2 %copy-start.4 = (f32[9,8192]{1,0:T(8,128)S(1)}, f32[9,8192]{1,0:T(8,128)}, u32[]{:S(2)}) copy-start(f32[9,8192]{1,0:T(8,128)} %tile_old.1) | copy-start | bytes 884740
  7.9 4.2 %copy-start.5 = (f32[9,8192]{1,0:T(8,128)S(1)}, f32[9,8192]{1,0:T(8,128)}, u32[]{:S(2)}) copy-start(f32[9,8192]{1,0:T(8,128)} %tile_forcing.1) | copy-start | bytes 884740
  12.1 14.0 %copy-start.6 = (s32[8192]{0:T(1024)S(1)}, s32[8192]{0:T(1024)}, u32[]{:S(2)}) copy-start(s32[8192]{0:T(1024)} %param.13) | copy-start | bytes 98308
  12.1 14.0 %copy-start.7 = (f32[8192]{0:T(1024)S(1)}, f32[8192]{0:T(1024)}, u32[]{:S(2)}) copy-start(f32[8192]{0:T(1024)} %param.12) | copy-start | bytes 98308

commit v3 on v2

--- a/solution.py
+++ b/solution.py
@@ -7,12 +7,14 @@
 from jax.experimental.pallas import tpu as pltpu
 from jax.sharding import PartitionSpec as P
 
+
 ITERS = 8
 LANES = 128
 SUB = 8
 GRANT = 16 * 1024 * 1024
 WIDE_GRANT = 55 * 1024 * 1024
-HIGH = lax.Precision.HIGHEST
+EDGE_GRANT = 60 * 1024 * 1024
+TILE_GRANT = 48 * 1024 * 1024
 F32 = jnp.float32
 I32 = jnp.int32
 VMEM = pltpu.VMEM
@@ -55,8 +57,22 @@
     return jnp.where(condition, jnp.ones((), F32), jnp.zeros((), F32))
 
 
-def dot(a, b):
-    return jnp.dot(a, b, precision=HIGH, preferred_element_type=F32)
+def spread(values):
+    high = values.astype(jnp.bfloat16)
+    rest = values - high.astype(F32)
+    middle = rest.astype(jnp.bfloat16)
+    low = (rest - middle.astype(F32)).astype(jnp.bfloat16)
+    return jnp.concatenate([high, middle, low], axis=0)
+
+
+def select_rows(chooser, values):
+    return jnp.dot(chooser, spread(values), preferred_element_type=F32)
+
+
+def count_dot(a, b):
+    return jnp.dot(
+        a.astype(jnp.bfloat16), b.astype(jnp.bfloat16), preferred_element_type=F32
+    )
 
 
 def lane_of(position, fast):
@@ -93,10 +109,10 @@
     shape = (rows, LANES)
     land = mask.astype(F32)
     upper = one_hot(row_index((LANES, LANES)) <= lane_index((LANES, LANES)))
-    running = dot(land, upper)
-    totals = dot(land, jnp.ones((LANES, LANES), F32))
+    running = count_dot(land, upper)
+    totals = count_dot(land, jnp.ones((LANES, LANES), F32))
     before = one_hot(lane_index((rows, rows)) < row_index((rows, rows)))
-    base = dot(before, totals).astype(I32)
+    base = count_dot(before, totals).astype(I32)
     totals = totals.astype(I32)
     running = running.astype(I32)
     start = base & (LANES - 1)
@@ -113,55 +129,51 @@
     first_ref[...] = one_hot(valid & (position >= start))
     second_ref[...] = one_hot(valid & (position < start))
     row_totals = lax.dot_general(
-        jnp.ones((SUB, LANES), F32),
-        land,
+        jnp.ones((SUB, LANES), jnp.bfloat16),
+        land.astype(jnp.bfloat16),
         (((1,), (1,)), ((), ())),
-        precision=HIGH,
         preferred_element_type=F32,
     )
     earlier = one_hot(row_index((rows, rows)) < lane_index((rows, rows)))
-    base_row = dot(row_totals, earlier).astype(I32)[:1]
+    base_row = count_dot(row_totals, earlier).astype(I32)[:1]
     lead_row = jnp.broadcast_to(base_row >> 7, (rows, rows))
     wanted = rank_row_of(row_index((rows, rows)), fast)
     place_ref[...] = jnp.concatenate(
-        [one_hot(lead_row == wanted), one_hot(lead_row + 1 == wanted)], axis=1
-    )
+        [one_hot(lead_row == wanted), one_hot(lead_row + 1 == wanted)] * 3, axis=1
+    ).astype(jnp.bfloat16)
     lead = (base >> 7)[:, :rows] if rows <= LANES else base[:, :1] >> 7
     held = rank_row_of(lane_index((rows, rows)), fast)
-    fetch_ref[...] = jnp.concatenate(
-        [one_hot(lead == held), one_hot(lead + 1 == held)], axis=0
-    )
+    chooser = jnp.concatenate([one_hot(lead == held), one_hot(lead + 1 == held)], axis=0)
+    fetch_ref[...] = jnp.concatenate([chooser] * 3, axis=1).astype(jnp.bfloat16)
     spot = start + running - 1
     spot_ref[...] = lane_of(spot & (LANES - 1), fast) + (spot & LANES)
 
 
+def cut_edges(parity, coupling, next_edge, pair_edge, low, high, sems):
+    columns = coupling.shape[1]
+    copies = [
+        pltpu.make_async_copy(coupling.at[:, pl.ds(0, LANES)], low, sems.at[0]),
+        pltpu.make_async_copy(coupling.at[:, pl.ds(columns - LANES, LANES)], high, sems.at[1]),
+    ]
+    for copy in copies:
+        copy.start()
+    for copy in copies:
+        copy.wait()
+    even = parity[0] == 0
+    next_edge[...] = jnp.where(even, low[...], high[...])
+    pair_edge[...] = jnp.where(even, high[...], low[...])
+
+
 def prepare(
-    fast,
-    coupling,
-    column_old,
-    mask,
-    smooth,
-    old,
-    source,
-    first,
-    second,
-    place,
-    fetch,
-    spot,
-    padded,
-    sem_coupling,
-    sem_old,
+    fast, coupling, mask, padded, source, first, second, place, fetch, spot, held, sem, mask_sem
 ):
-    levels, rows, lanes = smooth.shape
-    blocks = rows // SUB
-    inner = padded.at[:, pl.ds(SUB, rows), :]
+    levels, height, _ = padded.shape
+    rows = height - 2 * SUB
+    mask_copy = pltpu.make_async_copy(mask, held, mask_sem)
+    mask_copy.start()
     for t in range(rows):
         pltpu.make_async_copy(
-            coupling.at[:, pl.ds(t * LANES, LANES)], padded.at[:, SUB + t, :], sem_coupling
-        ).start()
-    for t in range(rows):
-        pltpu.make_async_copy(
-            column_old.at[:, pl.ds(t * LANES, LANES)], old.at[:, t, :], sem_old
+            coupling.at[:, pl.ds(t * LANES, LANES)], padded.at[:, SUB + t, :], sem
         ).start()
     blank = jnp.zeros((SUB, LANES), F32)
 
@@ -171,30 +183,16 @@
         return carried
 
     lax.fori_loop(0, levels, clear, 0, unroll=3)
-    build_tables(fast, mask[...], source, first, second, place, fetch, spot)
-    lane = lane_index((SUB, LANES))
-    at_last = lane == LANES - 1
-    at_first = lane == 0
-    pltpu.make_async_copy(inner, inner, sem_coupling).wait()
-
-    def smooth_level(level, carried):
-        for g in range(blocks):
-            here = padded[level, pl.ds(SUB + g * SUB, SUB), :]
-            above = padded[level, pl.ds(SUB + g * SUB - 1, SUB), :]
-            below = padded[level, pl.ds(SUB + g * SUB + 1, SUB), :]
-            left = pltpu.roll(jnp.where(at_last, above, here), 1, 1)
-            right = pltpu.roll(jnp.where(at_first, below, here), LANES - 1, 1)
-            smooth[level, pl.ds(g * SUB, SUB), :] = (left + 2.0 * here + right) * 0.25
-        return carried
-
-    lax.fori_loop(0, levels, smooth_level, 0, unroll=levels // 3)
-    pltpu.make_async_copy(old, old, sem_old).wait()
+    mask_copy.wait()
+    build_tables(fast, held[...], source, first, second, place, fetch, spot)
+    inner = padded.at[:, pl.ds(SUB, rows), :]
+    pltpu.make_async_copy(inner, inner, sem).wait()
 
 
 def eliminate(
     fast,
     parity,
-    smooth,
+    padded,
     old,
     pair_edge,
     next_edge,
@@ -225,7 +223,8 @@
     forcing,
     sems,
 ):
-    levels, rows, lanes = smooth.shape
+    levels, height, _ = padded.shape
+    rows = height - 2 * SUB
     blocks = rows // SUB
     copies = [
         pltpu.make_async_copy(source_tile, buffer, sems.at[n])
@@ -249,18 +248,29 @@
     row, lane = row_index((SUB, LANES)), lane_index((SUB, LANES))
     low_corner = (row == 0) & (lane == 0)
     high_corner = (row == SUB - 1) & (lane == LANES - 1)
+    at_last, at_first = lane == LANES - 1, lane == 0
     blank = jnp.zeros((SUB, LANES), F32)
 
     def smooth_at(level):
-        values = [smooth[level, pl.ds(g * SUB, SUB), :] for g in range(blocks)]
+        values = []
+        for g in range(blocks):
+            top = SUB + g * SUB
+            here = padded[level, pl.ds(top, SUB), :]
+            above = padded[level, pl.ds(top - 1, SUB), :]
+            below = padded[level, pl.ds(top + 1, SUB), :]
+            left = pltpu.roll(jnp.where(at_last, above, here), 1, 1)
+            right = pltpu.roll(jnp.where(at_first, below, here), LANES - 1, 1)
+            values.append((left + 2.0 * here + right) * 0.25)
         low = jnp.broadcast_to(low_edge[pl.ds(level, 1), :], (SUB, LANES))
         high = jnp.broadcast_to(high_edge[pl.ds(level, 1), :], (SUB, LANES))
         values[0] = values[0] + jnp.where(low_corner, low, blank)
         values[-1] = values[-1] + jnp.where(high_corner, high, blank)
         return values
 
-    def step(count, carried):
-        level = levels - count
+    def old_at(level, g):
+        return old[level, pl.ds(g * SUB * LANES, SUB * LANES)].reshape(SUB, LANES)
+
+    def step(level, carried):
         conduct_u, right_n = carried
         below = smooth_at(level - 1)
         next_u, next_n = [], []
@@ -270,16 +280,18 @@
             offset[level - 2, pl.ds(g * SUB, SUB), :] = e
             factor[level - 2, pl.ds(g * SUB, SUB), :] = below[g] * inverse
             next_u.append(1.0 + (below[g] * conduct_u[g]) * inverse)
-            next_n.append(old[level - 1, pl.ds(g * SUB, SUB), :] + below[g] * e)
+            next_n.append(old_at(level - 1, g) + below[g] * e)
         return next_u, next_n
 
-    top = [old[levels, pl.ds(g * SUB, SUB), :] for g in range(blocks)]
+    top = [old_at(levels, g) for g in range(blocks)]
     ones = [jnp.ones((SUB, LANES), F32) for _ in range(blocks)]
-    conduct_u, right_n = lax.fori_loop(0, levels - 1, step, (ones, top), unroll=2)
+    conduct_u, right_n = ones, top
+    for level in range(levels, 1, -1):
+        conduct_u, right_n = step(level, (conduct_u, right_n))
     ground = smooth_at(0)
     for g in range(blocks):
         here = pl.ds(g * SUB, SUB)
-        params[0, here, :] = old[0, here, :]
+        params[0, here, :] = old_at(0, g)
         params[1, here, :] = right_n[g]
         params[2, here, :] = conduct_u[g]
         params[3, here, :] = ground[g]
@@ -317,7 +329,7 @@
     for n in range(4):
         moved = jnp.take_along_axis(params[n], pick, axis=1)
         halves.append(jnp.concatenate([moved * lead, moved * rest], axis=0))
-    packed = dot(place[...], jnp.concatenate(halves, axis=1))
+    packed = select_rows(place[...], jnp.concatenate(halves, axis=1))
     for n in range(4):
         field = packed[:, n * LANES : (n + 1) * LANES]
         if fast:
@@ -354,9 +366,8 @@
     sems,
     tile_sem,
 ):
-    upper, rows, lanes = offset.shape
+    upper, rows, _ = offset.shape
     blocks = rows // SUB
-    levels = upper + 2
     tiles = tile_base.shape[0]
     fields = []
     for n in range(2):
@@ -366,7 +377,7 @@
             )
         else:
             fields.append(inbox[n])
-    windows = dot(fetch[...], jnp.concatenate(fields, axis=1))
+    windows = select_rows(fetch[...], jnp.concatenate(fields, axis=1))
     place = spot[...]
     lane, upper_half = place & (LANES - 1), place >= LANES
     is_land = mask[...] == 1
@@ -378,49 +389,50 @@
             jnp.take_along_axis(two, lane, axis=1),
             jnp.take_along_axis(one, lane, axis=1),
         )
-        solved[n, pl.ds(0, rows), :] = jnp.where(is_land, found, ocean)
-        solved[n, pl.ds(rows, rows), :] = land[n]
-    for n in range(4):
-        solved[2 + n, pl.ds(0, rows), :] = params[n]
-        for i in range(blocks):
-            got = inbox[i, 2 + n] if fast else slots[n, pl.ds(i * SUB, SUB), :]
-            solved[2 + n, pl.ds(rows + i * SUB, SUB), :] = got
-    everything = 2 * blocks
-
-    def iterate(repeat, flux):
+        solved[n] = jnp.where(is_land, found, ocean)
+
+    def update(a, b, base, n1, w, ground, flux):
+        k = ground * (1.0 + 0.5 * jnp.tanh(flux))
+        total = w + k
+        surface = ((base + a) * total + k * n1) * reciprocal((1.0 + b) * total + w * k)
+        return k, surface, a - b * surface
+
+    zero = jnp.zeros((SUB, LANES), F32)
+    spans = [pl.ds(g * SUB, SUB) for g in range(blocks)]
+
+    def over_columns(repeat, flux):
         fluxes = []
-        for g in range(everything):
-            here = pl.ds(g * SUB, SUB)
-            a, b = solved[0, here, :], solved[1, here, :]
-            base, n1, w, ground = (solved[2 + n, here, :] for n in range(4))
-            if g >= blocks:
-                w = jnp.where(ground > 0.0, w, 1.0)
-            k = ground * (1.0 + 0.5 * jnp.tanh(flux[g]))
-            total = w + k
-            top = (base + a) * total + k * n1
-            bottom = (1.0 + b) * total + w * k
-            surface = top * reciprocal(bottom)
-            if g >= blocks:
-                warm[pl.ds((g - blocks) * SUB, SUB), :] = jnp.where(ground > 0.0, surface, 0.0)
-            else:
-                column_buffer[0, here, :] = surface
-                column_buffer[1, here, :] = k
-            fluxes.append(a - b * surface)
+        for here, last in zip(spans, flux):
+            k, surface, next_flux = update(
+                solved[0, here, :], solved[1, here, :], *(params[n, here, :] for n in range(4)), last
+            )
+            column_buffer[0, here, :] = surface
+            column_buffer[1, here, :] = k
+            fluxes.append(next_flux)
         return fluxes
 
-    zero = jnp.zeros((SUB, LANES), F32)
-    lax.fori_loop(0, ITERS, iterate, [zero] * everything)
-    for t in range(tiles):
-        tile_buffer[t] = tile_base[t] + tile_slope[t] * warm[...]
-    for t in range(rows):
-        pltpu.make_async_copy(
-            tile_buffer.at[:, t, :], tile_temp.at[:, pl.ds(t * LANES, LANES)], tile_sem
-        ).start()
+    def land_params(i):
+        return [inbox[i, 2 + n] if fast else slots[n, spans[i], :] for n in range(4)]
+
+    def over_land(repeat, flux):
+        fluxes = []
+        for i, (here, last) in enumerate(zip(spans, flux)):
+            base, n1, w, ground = land_params(i)
+            w = jnp.where(ground > 0.0, w, 1.0)
+            _, surface, next_flux = update(
+                land[0, here, :], land[1, here, :], base, n1, w, ground, last
+            )
+            warm[here, :] = surface
+            fluxes.append(next_flux)
+        return fluxes
+
     width = 2
-    for part in range(blocks // width):
-        spans = [pl.ds((part * width + g) * SUB, SUB) for g in range(width)]
+    parts = blocks // width
+
+    def solve_columns(part):
+        chosen = spans[part * width : (part + 1) * width]
         values = []
-        for here in spans:
+        for here in chosen:
             surface, k = column_buffer[0, here, :], column_buffer[1, here, :]
             n1, w = params[1, here, :], params[2, here, :]
             value = (n1 + k * surface) * reciprocal(w + k)
@@ -430,21 +442,37 @@
         def substitute(level, values):
             values = [
                 offset[level, here, :] + factor[level, here, :] * value
-                for here, value in zip(spans, values)
+                for here, value in zip(chosen, values)
             ]
-            for here, value in zip(spans, values):
+            for here, value in zip(chosen, values):
                 column_buffer[level + 2, here, :] = value
             return values
 
-        lax.fori_loop(0, upper, substitute, values, unroll=4)
+        lax.fori_loop(0, upper, substitute, values, unroll=upper // 4)
         for t in range(part * width * SUB, (part + 1) * width * SUB):
             pltpu.make_async_copy(
                 column_buffer.at[:, t, :],
                 column_temp.at[:, pl.ds(t * LANES, LANES)],
                 sems.at[part],
             ).start()
+
+    lax.fori_loop(0, ITERS, over_columns, [zero] * blocks, unroll=2)
+    early = min(2, parts)
+    for part in range(early):
+        solve_columns(part)
+    lax.fori_loop(0, ITERS, over_land, [zero] * blocks, unroll=2)
+    for i, here in enumerate(spans):
+        surface = jnp.where(land_params(i)[3] > 0.0, warm[here, :], zero)
+        for t in range(tiles):
+            tile_buffer[t, here, :] = tile_base[t, here, :] + tile_slope[t, here, :] * surface
+    for t in range(rows):
+        pltpu.make_async_copy(
+            tile_buffer.at[:, t, :], tile_temp.at[:, pl.ds(t * LANES, LANES)], tile_sem
+        ).start()
+    for part in range(early, parts):
+        solve_columns(part)
     pltpu.make_async_copy(tile_buffer, tile_buffer, tile_sem).wait()
-    for part in range(blocks // width):
+    for part in range(parts):
         span = column_buffer.at[:, pl.ds(part * width * SUB, width * SUB), :]
         pltpu.make_async_copy(span, span, sems.at[part]).wait()
 
@@ -472,13 +500,8 @@
     fast = peers == SUB and rows == SUB * SUB
     devices = peers * lax.axis_size("lev")
     parity = lax.rem(lax.axis_index(axes), 2)
-    first_edge, last_edge = coupling[:, :LANES], coupling[:, columns - LANES :]
-    even = parity == 0
     pairs = [(i, i ^ 1) for i in range(devices)]
     following = [(i, (i + 1 if i % 2 else i - 1) % devices) for i in range(devices)]
-    next_edge = lax.ppermute(jnp.where(even, first_edge, last_edge), axes, following)
-    pair_edge = lax.ppermute(jnp.where(even, last_edge, first_edge), axes, pairs)
-
     hbm, vmem, smem = pl.ANY, pltpu.VMEM, pltpu.SMEM
     full = (rows, LANES)
     mask = land_mask.reshape(full)
@@ -486,17 +509,30 @@
         VMEM(full, I32),
         VMEM(full, F32),
         VMEM(full, F32),
-        VMEM((rows, 2 * rows), F32),
-        VMEM((2 * rows, rows), F32),
+        VMEM((rows, 6 * rows), jnp.bfloat16),
+        VMEM((2 * rows, 3 * rows), jnp.bfloat16),
         VMEM(full, I32),
     ]
-    smooth, old, source, first, second, place, fetch, spot = chip_call(
+    edge = (couplings, LANES)
+    next_own, pair_own = chip_call(
+        cut_edges,
+        [VMEM(edge, F32)] * 2,
+        [smem, pltpu.HBM],
+        [vmem] * 2,
+        [VMEM(edge, F32)] * 2 + [DMA((2,))],
+        (parity.reshape(1), coupling),
+        pl.CostEstimate(flops=0, bytes_accessed=16 * couplings * LANES, transcendentals=0),
+        EDGE_GRANT,
+    )
+    next_edge = lax.ppermute(next_own, axes, following)
+    pair_edge = lax.ppermute(pair_own, axes, pairs)
+    padded, source, first, second, place, fetch, spot = chip_call(
         functools.partial(prepare, fast),
-        [VMEM((couplings,) + full, F32), VMEM((levels,) + full, F32)] + table_outs,
-        [hbm, hbm, vmem],
-        [vmem] * 8,
-        [VMEM((couplings, rows + 2 * SUB, LANES), F32), DMA, DMA],
-        (coupling, column_old, mask),
+        [VMEM((couplings, rows + 2 * SUB, LANES), F32)] + table_outs,
+        [pltpu.HBM] * 2,
+        [vmem] * 7,
+        [VMEM(full, I32), DMA, DMA],
+        (coupling, mask),
         pl.CostEstimate(
             flops=8 * couplings * columns, bytes_accessed=8 * levels * columns, transcendentals=0
         ),
@@ -515,13 +551,13 @@
             VMEM((tiles,) + full, F32),
             handed(sent, F32),
         ],
-        [smem] + [vmem] * 8 + [hbm] * 6,
+        [smem] + [vmem] * 8 + [pltpu.HBM] * 6,
         [vmem] * 7,
         [VMEM((couplings, LANES), F32)] * 2 + [VMEM((tiles, columns), F32)] * 6 + [DMA((6,))],
         (
             parity.reshape(1),
-            smooth,
-            old,
+            padded,
+            on_chip(column_old),
             pair_edge,
             next_edge,
             source,
@@ -538,6 +574,7 @@
         pl.CostEstimate(
             flops=20 * levels * columns, bytes_accessed=24 * tiles * columns, transcendentals=0
         ),
+        TILE_GRANT,
     )
     if fast:
         inbox = lax.all_to_all(send, "lon", split_axis=0, concat_axis=0, tiled=True)
@@ -560,7 +597,7 @@
         [vmem] * 12,
         [hbm, hbm],
         [
-            VMEM((6, 2 * rows, LANES), F32),
+            VMEM((2,) + full, F32),
             VMEM(full, F32),
             VMEM((levels,) + full, F32),
             VMEM((tiles,) + full, F32),

time: 29.6 us -> 27.6 us (0.932)
  Pallas kernels: 10.1 us -> 8.56 us
  other arithmetic: 0.8 us -> 0 us
  starting transfers between devices: 6.4 us -> 7.14 us
  blocking collectives: 11.3 us -> 10.8 us
    pallas_call x3 -> x4, Pallas kernels: 10.1 us -> 8.56 us  [chip_call(): pl.pallas_call(kernel, out_shape=outs, in_specs=[pl.BlockSpec(memory_spac...]
    select_n x1 -> x0, other arithmetic: 0.8 us -> none  [on_device(): jnp.where(even, first_edge, last_edge)]
    ppermute x2, starting transfers between devices: 6.4 us -> 7.14 us  [the longest x1 6.58 us: on_device(): next_edge = lax.ppermute(next_own, axes, following)]
    all_to_all x1, blocking collectives: 11.3 us -> 10.8 us  [on_device(): inbox = lax.all_to_all(send, 'lon', split_axis=0, concat_axis=0, tiled=True)]
  transfers between devices with their start and end apart: 2 -> 2, of which waited for: 0 -> 0; matrix products, arithmetic and copies ran while one was open for 0% -> 0% of each run, Pallas kernels for 14% -> 7%
where the time goes in v3:
time: 27.6 us; the launch traced here: 27.2 us
  blocking collectives  10.8 us (39%)
  Pallas kernels  8.56 us (31%)
  starting transfers between devices  7.14 us (26%)
  between operations  0.71 us (3%)
    all_to_all x1, blocking collectives, on_device(): inbox = lax.all_to_all(send, 'lon', split_axis=0, concat_axis=0, tiled=True)  10.8 us
    pallas_call x4, Pallas kernels, chip_call(): pl.pallas_call(kernel, out_shape=outs, in_specs=[pl.BlockSpec(memory_spac...  8.56 us
    ppermute x1, starting transfers between devices, on_device(): next_edge = lax.ppermute(next_own, axes, following)  6.58 us
    ppermute x1, starting transfers between devices, on_device(): pair_edge = lax.ppermute(pair_own, axes, pairs)  0.56 us
  transfers between devices with their start and end apart: 2, of which 0 were waited for; matrix products, arithmetic and copies ran while one was open for 0% of the time, Pallas kernels for 7%

profile of v3, /device:TPU:0, one launch (start us, length us, event | category | flops | bytes accessed | tf_op | source)
XLA Modules:
  0.0 27.2 jit_solution(17098481519387503146)
XLA Ops:
  0.6 0.0 copy-start
  0.6 1.0 %shard_map.114 = (f32[69,128]{1,0:T(8,128)S(1)}, f32[69,128]{1,0:T(8,128)S(1)}) custom-call(s32[1]{0:T(128)} %bitcast.parity, f32[69,8192]{1,0:T(8,128)} %coupling.3), custom_call_target="tpu_custom_call" | custom-call | bytes 141312 | tf_op jit(solution)/shard_map/pallas_call | solution.py:29
  1.6 0.6 %collective-permute-start = (f32[69,128]{1,0:T(8,128)S(1)}, f32[69,128]{1,0:T(8,128)S(1)}, u32[]{:S(2)}, u32[]{:S(2)}) collective-permute-start(f32[69,128]{1,0:T(8,128)S(1)} %get-tuple-element.19), channel_id=1, source_target_pairs={{0,1},{1,0},{2,3},{3,2},{4,5},{5,4},{6,7},{7,6},{8,9},{9,8},{10,11... | collective-permute-start | bytes 105992 | tf_op jit(solution)/shard_map/ppermute | solution.py:528
  2.2 6.6 %collective-permute-start.1 = (f32[69,128]{1,0:T(8,128)S(1)}, f32[69,128]{1,0:T(8,128)S(1)}, u32[]{:S(2)}, u32[]{:S(2)}) collective-permute-start(f32[69,128]{1,0:T(8,128)S(1)} %get-tuple-element.20), channel_id=1, source_target_pairs={{0,31},{1,2},{2,1},{3,4},{4,3},{5,6},{6,5},{7,8},{8,7},{9,10},{10,... | collective-permute-start | bytes 105992 | tf_op jit(solution)/shard_map/ppermute | solution.py:527
  8.8 1.8 %shard_map.113 = (f32[69,80,128]{2,1,0:T(8,128)S(1)}, s32[64,128]{1,0:T(8,128)S(1)}, f32[64,128]{1,0:T(8,128)S(1)}, f32[64,128]{1,0:T(8,128)S(1)}, bf16[64,384]{...) custom-call(f32[69,8192]{1,0:T(8,128)} %coupling.3, s32[64,128]{1,0:T(8,128)} %bitcast.3), custom_call_target="tpu_custom_call" | custom-call | flops 4521984 | bytes 4587520 | tf_op jit(solution)/shard_map/pallas_call | solution.py:29
  10.6 0.0 collective-permute-done.pair_edge
  10.6 0.0 collective-permute-done.1.next_edge
  10.6 0.0 copy-done
  10.6 0.0 copy-start.1
  10.6 0.0 copy-start.2
  10.6 2.8 %shard_map.115 = (f32[68,64,128]{2,1,0:T(8,128)S(1)}, f32[68,64,128]{2,1,0:T(8,128)S(1)}, f32[4,64,128]{2,1,0:T(8,128)S(1)}, f32[2,64,128]{2,1,0:T(8,128)S(1)}, ...) custom-call(s32[1]{0:T(128)} %bitcast.parity, ...), custom_call_target="tpu_custom_call" | custom-call | flops 11468800 | bytes 1769472 | tf_op jit(solution)/shard_map/pallas_call | solution.py:29
  13.5 10.8 %all_to_all.5.inbox.slots = f32[8,6,8,128]{3,2,1,0:T(8,128)S(1)} all-to-all(f32[8,6,8,128]{3,2,1,0:T(8,128)S(1)} %get-tuple-element.25), channel_id=1, replica_groups=mesh['lon'=8,'lev'=4] {'lon'}, dimensions={0} | all-to-all | bytes 393216 | tf_op jit(solution)/shard_map/all_to_all | solution.py:580
  24.3 0.0 copy-done.1
  24.3 0.0 copy-done.2
  24.3 3.0 %shard_map.116 = (f32[70,8192]{1,0:T(8,128)}, f32[9,8192]{1,0:T(8,128)}) custom-call(f32[8,6,8,128]{3,2,1,0:T(8,128)S(1)} %all_to_all.5.inbox.slots, f32[8,6,8,128]{3,2,1,0:T(8,128)S(1)} %all_to_all.5.inbox.slots, f32[68,64,128]{2,1,0:T(8,128)S(1)} %get-tuple-element.26.offset, f32[68,64,128]{2,1,0:T(8,128)S(1)} %get-tuple-element.27.factor, ...), custom_call_target="tpu_custom_call" | custom-call | flops 2293760 | bytes 2293760 | tf_op jit(solution)/shard_map/pallas_call | solution.py:29
Async XLA Ops:
  0.6 10.0 %copy-start = (f32[70,8192]{1,0:T(8,128)S(1)}, f32[70,8192]{1,0:T(8,128)}, u32[]{:S(2)}) copy-start(f32[70,8192]{1,0:T(8,128)} %old.1) | copy-start | bytes 6881284
  1.6 9.0 %collective-permute-start = (f32[69,128]{1,0:T(8,128)S(1)}, f32[69,128]{1,0:T(8,128)S(1)}, u32[]{:S(2)}, u32[]{:S(2)}) collective-permute-start(f32[69,128]{1,0:T(8,128)S(1)} %get-tuple-element.19), channel_id=1, source_target_pairs={{0,1},{1,0},{2,3},{3,2},{4,5},{5,4},{6,7},{7,6},{8,9},{9,8},{10,11... | collective-permute-start | bytes 105992 | tf_op jit(solution)/shard_map/ppermute | solution.py:528
  2.2 8.4 %collective-permute-start.1 = (f32[69,128]{1,0:T(8,128)S(1)}, f32[69,128]{1,0:T(8,128)S(1)}, u32[]{:S(2)}, u32[]{:S(2)}) collective-permute-start(f32[69,128]{1,0:T(8,128)S(1)} %get-tuple-element.20), channel_id=1, source_target_pairs={{0,31},{1,2},{2,1},{3,4},{4,3},{5,6},{6,5},{7,8},{8,7},{9,10},{10,... | collective-permute-start | bytes 105992 | tf_op jit(solution)/shard_map/ppermute | solution.py:527
  10.6 13.6 %copy-start.1 = (s32[8192]{0:T(1024)S(1)}, s32[8192]{0:T(1024)}, u32[]{:S(2)}) copy-start(s32[8192]{0:T(1024)} %param.13) | copy-start | bytes 98308
  10.6 13.6 %copy-start.2 = (f32[8192]{0:T(1024)S(1)}, f32[8192]{0:T(1024)}, u32[]{:S(2)}) copy-start(f32[8192]{0:T(1024)} %param.12) | copy-start | bytes 98308

commit v4 on v3

--- a/solution.py
+++ b/solution.py
@@ -13,7 +13,7 @@
 SUB = 8
 GRANT = 16 * 1024 * 1024
 WIDE_GRANT = 55 * 1024 * 1024
-EDGE_GRANT = 60 * 1024 * 1024
+EDGE_GRANT = 62 * 1024 * 1024
 TILE_GRANT = 48 * 1024 * 1024
 F32 = jnp.float32
 I32 = jnp.int32
@@ -260,7 +260,7 @@
             below = padded[level, pl.ds(top + 1, SUB), :]
             left = pltpu.roll(jnp.where(at_last, above, here), 1, 1)
             right = pltpu.roll(jnp.where(at_first, below, here), LANES - 1, 1)
-            values.append((left + 2.0 * here + right) * 0.25)
+            values.append((left + right) * 0.25 + here * 0.5)
         low = jnp.broadcast_to(low_edge[pl.ds(level, 1), :], (SUB, LANES))
         high = jnp.broadcast_to(high_edge[pl.ds(level, 1), :], (SUB, LANES))
         values[0] = values[0] + jnp.where(low_corner, low, blank)
@@ -278,9 +278,10 @@
             inverse = reciprocal(conduct_u[g] + below[g])
             e = right_n[g] * inverse
             offset[level - 2, pl.ds(g * SUB, SUB), :] = e
-            factor[level - 2, pl.ds(g * SUB, SUB), :] = below[g] * inverse
-            next_u.append(1.0 + (below[g] * conduct_u[g]) * inverse)
-            next_n.append(old_at(level - 1, g) + below[g] * e)
+            f = below[g] * inverse
+            factor[level - 2, pl.ds(g * SUB, SUB), :] = f
+            next_u.append(1.0 + f * conduct_u[g])
+            next_n.append(old_at(level - 1, g) + f * right_n[g])
         return next_u, next_n
 
     top = [old_at(levels, g) for g in range(blocks)]
@@ -323,7 +324,7 @@
         land[1, here, :] = land_b * inverse
         return carried
 
-    lax.fori_loop(0, blocks, tile_block, 0)
+    lax.fori_loop(0, blocks, tile_block, 0, unroll=True)
     pick, lead, rest = source[...], first[...], second[...]
     halves = []
     for n in range(4):

time: 27.6 us -> 27.4 us (level)
  no operation moved by 1% of the time
where the time goes in v4:
time: 27.4 us; the launch traced here: 27 us
  blocking collectives  10.8 us (39%)
  Pallas kernels  8.31 us (30%)
  starting transfers between devices  7.14 us (26%)
  between operations  0.71 us (3%)
    all_to_all x1, blocking collectives, on_device(): inbox = lax.all_to_all(send, 'lon', split_axis=0, concat_axis=0, tiled=True)  10.8 us
    pallas_call x4, Pallas kernels, chip_call(): pl.pallas_call(kernel, out_shape=outs, in_specs=[pl.BlockSpec(memory_spac...  8.31 us
    ppermute x1, starting transfers between devices, on_device(): next_edge = lax.ppermute(next_own, axes, following)  6.58 us
    ppermute x1, starting transfers between devices, on_device(): pair_edge = lax.ppermute(pair_own, axes, pairs)  0.56 us
  transfers between devices with their start and end apart: 2, of which 0 were waited for; matrix products, arithmetic and copies ran while one was open for 0% of the time, Pallas kernels for 7%

profile of v4, /device:TPU:0, one launch (start us, length us, event | category | flops | bytes accessed | tf_op | source)
XLA Modules:
  0.0 27.0 jit_solution(18047044951065199360)
XLA Ops:
  0.6 0.8 %shard_map.114 = (f32[69,128]{1,0:T(8,128)S(1)}, f32[69,128]{1,0:T(8,128)S(1)}) custom-call(s32[1]{0:T(128)} %bitcast.parity, f32[69,8192]{1,0:T(8,128)} %coupling.3), custom_call_target="tpu_custom_call" | custom-call | bytes 141312 | tf_op jit(solution)/shard_map/pallas_call | solution.py:29
  1.5 0.0 copy-start
  1.5 0.6 %collective-permute-start = (f32[69,128]{1,0:T(8,128)S(1)}, f32[69,128]{1,0:T(8,128)S(1)}, u32[]{:S(2)}, u32[]{:S(2)}) collective-permute-start(f32[69,128]{1,0:T(8,128)S(1)} %get-tuple-element.19), channel_id=1, source_target_pairs={{0,1},{1,0},{2,3},{3,2},{4,5},{5,4},{6,7},{7,6},{8,9},{9,8},{10,11... | collective-permute-start | bytes 105992 | tf_op jit(solution)/shard_map/ppermute | solution.py:529
  2.0 6.6 %collective-permute-start.1 = (f32[69,128]{1,0:T(8,128)S(1)}, f32[69,128]{1,0:T(8,128)S(1)}, u32[]{:S(2)}, u32[]{:S(2)}) collective-permute-start(f32[69,128]{1,0:T(8,128)S(1)} %get-tuple-element.20), channel_id=1, source_target_pairs={{0,31},{1,2},{2,1},{3,4},{4,3},{5,6},{6,5},{7,8},{8,7},{9,10},{10,... | collective-permute-start | bytes 105992 | tf_op jit(solution)/shard_map/ppermute | solution.py:528
  8.6 1.8 %shard_map.113 = (f32[69,80,128]{2,1,0:T(8,128)S(1)}, s32[64,128]{1,0:T(8,128)S(1)}, f32[64,128]{1,0:T(8,128)S(1)}, f32[64,128]{1,0:T(8,128)S(1)}, bf16[64,384]{...) custom-call(f32[69,8192]{1,0:T(8,128)} %coupling.3, s32[64,128]{1,0:T(8,128)} %bitcast.3), custom_call_target="tpu_custom_call" | custom-call | flops 4521984 | bytes 4587520 | tf_op jit(solution)/shard_map/pallas_call | solution.py:29
  10.4 0.0 collective-permute-done.pair_edge
  10.5 0.0 collective-permute-done.1.next_edge
  10.5 0.0 copy-done
  10.5 0.0 copy-start.1
  10.5 0.0 copy-start.2
  10.5 2.7 %shard_map.115 = (f32[68,64,128]{2,1,0:T(8,128)S(1)}, f32[68,64,128]{2,1,0:T(8,128)S(1)}, f32[4,64,128]{2,1,0:T(8,128)S(1)}, f32[2,64,128]{2,1,0:T(8,128)S(1)}, ...) custom-call(s32[1]{0:T(128)} %bitcast.parity, ...), custom_call_target="tpu_custom_call" | custom-call | flops 11468800 | bytes 1769472 | tf_op jit(solution)/shard_map/pallas_call | solution.py:29
  13.2 10.8 %all_to_all.5.inbox.slots = f32[8,6,8,128]{3,2,1,0:T(8,128)S(1)} all-to-all(f32[8,6,8,128]{3,2,1,0:T(8,128)S(1)} %get-tuple-element.25), channel_id=1, replica_groups=mesh['lon'=8,'lev'=4] {'lon'}, dimensions={0} | all-to-all | bytes 393216 | tf_op jit(solution)/shard_map/all_to_all | solution.py:581
  24.0 0.0 copy-done.1
  24.0 0.0 copy-done.2
  24.0 2.9 %shard_map.116 = (f32[70,8192]{1,0:T(8,128)}, f32[9,8192]{1,0:T(8,128)}) custom-call(f32[8,6,8,128]{3,2,1,0:T(8,128)S(1)} %all_to_all.5.inbox.slots, f32[8,6,8,128]{3,2,1,0:T(8,128)S(1)} %all_to_all.5.inbox.slots, f32[68,64,128]{2,1,0:T(8,128)S(1)} %get-tuple-element.26.offset, f32[68,64,128]{2,1,0:T(8,128)S(1)} %get-tuple-element.27.factor, ...), custom_call_target="tpu_custom_call" | custom-call | flops 2293760 | bytes 2293760 | tf_op jit(solution)/shard_map/pallas_call | solution.py:29
Async XLA Ops:
  1.5 9.0 %copy-start = (f32[70,8192]{1,0:T(8,128)S(1)}, f32[70,8192]{1,0:T(8,128)}, u32[]{:S(2)}) copy-start(f32[70,8192]{1,0:T(8,128)} %old.1) | copy-start | bytes 6881284
  1.5 9.0 %collective-permute-start = (f32[69,128]{1,0:T(8,128)S(1)}, f32[69,128]{1,0:T(8,128)S(1)}, u32[]{:S(2)}, u32[]{:S(2)}) collective-permute-start(f32[69,128]{1,0:T(8,128)S(1)} %get-tuple-element.19), channel_id=1, source_target_pairs={{0,1},{1,0},{2,3},{3,2},{4,5},{5,4},{6,7},{7,6},{8,9},{9,8},{10,11... | collective-permute-start | bytes 105992 | tf_op jit(solution)/shard_map/ppermute | solution.py:529
  2.0 8.4 %collective-permute-start.1 = (f32[69,128]{1,0:T(8,128)S(1)}, f32[69,128]{1,0:T(8,128)S(1)}, u32[]{:S(2)}, u32[]{:S(2)}) collective-permute-start(f32[69,128]{1,0:T(8,128)S(1)} %get-tuple-element.20), channel_id=1, source_target_pairs={{0,31},{1,2},{2,1},{3,4},{4,3},{5,6},{6,5},{7,8},{8,7},{9,10},{10,... | collective-permute-start | bytes 105992 | tf_op jit(solution)/shard_map/ppermute | solution.py:528
  10.5 13.5 %copy-start.1 = (s32[8192]{0:T(1024)S(1)}, s32[8192]{0:T(1024)}, u32[]{:S(2)}) copy-start(s32[8192]{0:T(1024)} %param.13) | copy-start | bytes 98308
  10.5 13.5 %copy-start.2 = (f32[8192]{0:T(1024)S(1)}, f32[8192]{0:T(1024)}, u32[]{:S(2)}) copy-start(f32[8192]{0:T(1024)} %param.12) | copy-start | bytes 98308

commit v5 on v4

--- a/solution.py
+++ b/solution.py
@@ -149,19 +149,23 @@
     spot_ref[...] = lane_of(spot & (LANES - 1), fast) + (spot & LANES)
 
 
-def cut_edges(parity, coupling, next_edge, pair_edge, low, high, sems):
-    columns = coupling.shape[1]
+def is_even():
+    return lax.rem(lax.axis_index("lon") * lax.axis_size("lev") + lax.axis_index("lev"), 2) == 0
+
+
+def cut_edges(coupling, next_edge, pair_edge, sems):
+    last = coupling.shape[1] - LANES
+    even = is_even()
+    near = pl.multiple_of(jnp.where(even, last, 0), LANES)
+    far = pl.multiple_of(jnp.where(even, 0, last), LANES)
     copies = [
-        pltpu.make_async_copy(coupling.at[:, pl.ds(0, LANES)], low, sems.at[0]),
-        pltpu.make_async_copy(coupling.at[:, pl.ds(columns - LANES, LANES)], high, sems.at[1]),
+        pltpu.make_async_copy(coupling.at[:, pl.ds(far, LANES)], next_edge, sems.at[0]),
+        pltpu.make_async_copy(coupling.at[:, pl.ds(near, LANES)], pair_edge, sems.at[1]),
     ]
     for copy in copies:
         copy.start()
     for copy in copies:
         copy.wait()
-    even = parity[0] == 0
-    next_edge[...] = jnp.where(even, low[...], high[...])
-    pair_edge[...] = jnp.where(even, high[...], low[...])
 
 
 def prepare(
@@ -191,7 +195,6 @@
 
 def eliminate(
     fast,
-    parity,
     padded,
     old,
     pair_edge,
@@ -241,10 +244,24 @@
     ]
     for copy in copies:
         copy.start()
-    even = parity[0] == 0
-    pair, following = pair_edge[...], next_edge[...]
-    low_edge[...] = pltpu.roll(jnp.where(even, following, pair), 1, 1) * 0.25
-    high_edge[...] = pltpu.roll(jnp.where(even, pair, following), LANES - 1, 1) * 0.25
+    even = is_even()
+
+    def turn(rows_here):
+        pair, following = pair_edge[rows_here, :], next_edge[rows_here, :]
+        low = jnp.where(even, following, pair)
+        high = jnp.where(even, pair, following)
+        low_edge[rows_here, :] = pltpu.roll(low, 1, 1) * 0.25
+        high_edge[rows_here, :] = pltpu.roll(high, LANES - 1, 1) * 0.25
+
+    half = levels // (2 * SUB) * SUB
+
+    def turn_half(index, carried):
+        turn(pl.ds(pl.multiple_of(index * half, SUB), half))
+        return carried
+
+    lax.fori_loop(0, 2, turn_half, 0)
+    if levels > 2 * half:
+        turn(pl.ds(2 * half, levels - 2 * half))
     row, lane = row_index((SUB, LANES)), lane_index((SUB, LANES))
     low_corner = (row == 0) & (lane == 0)
     high_corner = (row == SUB - 1) & (lane == LANES - 1)
@@ -296,6 +313,19 @@
         params[1, here, :] = right_n[g]
         params[2, here, :] = conduct_u[g]
         params[3, here, :] = ground[g]
+    pick, lead, rest = source[...], first[...], second[...]
+    halves = []
+    for n in range(4):
+        moved = jnp.take_along_axis(params[n], pick, axis=1)
+        halves.append(jnp.concatenate([moved * lead, moved * rest], axis=0))
+    packed = select_rows(place[...], jnp.concatenate(halves, axis=1))
+    for n in range(4):
+        field = packed[:, n * LANES : (n + 1) * LANES]
+        if fast:
+            for k, block in enumerate(exchange([field[g * SUB : (g + 1) * SUB] for g in range(blocks)])):
+                send[k, 2 + n] = block
+        else:
+            send[n] = field
     for copy in copies:
         copy.wait()
     tiles = weight.shape[0]
@@ -325,19 +355,6 @@
         return carried
 
     lax.fori_loop(0, blocks, tile_block, 0, unroll=True)
-    pick, lead, rest = source[...], first[...], second[...]
-    halves = []
-    for n in range(4):
-        moved = jnp.take_along_axis(params[n], pick, axis=1)
-        halves.append(jnp.concatenate([moved * lead, moved * rest], axis=0))
-    packed = select_rows(place[...], jnp.concatenate(halves, axis=1))
-    for n in range(4):
-        field = packed[:, n * LANES : (n + 1) * LANES]
-        if fast:
-            for k, block in enumerate(exchange([field[g * SUB : (g + 1) * SUB] for g in range(blocks)])):
-                send[k, 2 + n] = block
-        else:
-            send[n] = field
     if fast:
         for k in range(blocks):
             for n in range(2):
@@ -500,10 +517,9 @@
     blocks = rows // SUB
     fast = peers == SUB and rows == SUB * SUB
     devices = peers * lax.axis_size("lev")
-    parity = lax.rem(lax.axis_index(axes), 2)
     pairs = [(i, i ^ 1) for i in range(devices)]
     following = [(i, (i + 1 if i % 2 else i - 1) % devices) for i in range(devices)]
-    hbm, vmem, smem = pl.ANY, pltpu.VMEM, pltpu.SMEM
+    hbm, vmem = pl.ANY, pltpu.VMEM
     full = (rows, LANES)
     mask = land_mask.reshape(full)
     table_outs = [
@@ -518,10 +534,10 @@
     next_own, pair_own = chip_call(
         cut_edges,
         [VMEM(edge, F32)] * 2,
-        [smem, pltpu.HBM],
+        [pltpu.HBM],
         [vmem] * 2,
-        [VMEM(edge, F32)] * 2 + [DMA((2,))],
-        (parity.reshape(1), coupling),
+        [DMA((2,))],
+        (coupling,),
         pl.CostEstimate(flops=0, bytes_accessed=16 * couplings * LANES, transcendentals=0),
         EDGE_GRANT,
     )
@@ -552,11 +568,10 @@
             VMEM((tiles,) + full, F32),
             handed(sent, F32),
         ],
-        [smem] + [vmem] * 8 + [pltpu.HBM] * 6,
+        [vmem] * 8 + [pltpu.HBM] * 6,
         [vmem] * 7,
         [VMEM((couplings, LANES), F32)] * 2 + [VMEM((tiles, columns), F32)] * 6 + [DMA((6,))],
         (
-            parity.reshape(1),
             padded,
             on_chip(column_old),
             pair_edge,

time: 27.4 us -> 27.1 us (0.989)
  Pallas kernels: 8.31 us -> 8.03 us
    pallas_call x4, Pallas kernels: 8.31 us -> 8.03 us  [chip_call(): pl.pallas_call(kernel, out_shape=outs, in_specs=[pl.BlockSpec(memory_spac...]
where the time goes in v5:
time: 27.1 us; the launch traced here: 26.7 us
  blocking collectives  10.8 us (40%)
  Pallas kernels  8.03 us (30%)
  starting transfers between devices  7.14 us (26%)
  between operations  0.7 us (3%)
    all_to_all x1, blocking collectives, on_device(): inbox = lax.all_to_all(send, 'lon', split_axis=0, concat_axis=0, tiled=True)  10.8 us
    pallas_call x4, Pallas kernels, chip_call(): pl.pallas_call(kernel, out_shape=outs, in_specs=[pl.BlockSpec(memory_spac...  8.03 us
    ppermute x1, starting transfers between devices, on_device(): next_edge = lax.ppermute(next_own, axes, following)  6.58 us
    ppermute x1, starting transfers between devices, on_device(): pair_edge = lax.ppermute(pair_own, axes, pairs)  0.56 us
  transfers between devices with their start and end apart: 2, of which 0 were waited for; matrix products, arithmetic and copies ran while one was open for 0% of the time, Pallas kernels for 7%

profile of v5, /device:TPU:0, one launch (start us, length us, event | category | flops | bytes accessed | tf_op | source)
XLA Modules:
  0.0 26.7 jit_solution(15237759225127804540)
XLA Ops:
  0.6 0.8 %shard_map.114 = (f32[69,128]{1,0:T(8,128)S(1)}, f32[69,128]{1,0:T(8,128)S(1)}) custom-call(f32[69,8192]{1,0:T(8,128)} %coupling.3), custom_call_target="tpu_custom_call" | custom-call | bytes 141312 | tf_op jit(solution)/shard_map/pallas_call | solution.py:29
  1.5 0.0 copy-start
  1.5 0.6 %collective-permute-start = (f32[69,128]{1,0:T(8,128)S(1)}, f32[69,128]{1,0:T(8,128)S(1)}, u32[]{:S(2)}, u32[]{:S(2)}) collective-permute-start(f32[69,128]{1,0:T(8,128)S(1)} %get-tuple-element.19), channel_id=1, source_target_pairs={{0,1},{1,0},{2,3},{3,2},{4,5},{5,4},{6,7},{7,6},{8,9},{9,8},{10,11... | collective-permute-start | bytes 105992 | tf_op jit(solution)/shard_map/ppermute | solution.py:545
  2.0 6.6 %collective-permute-start.1 = (f32[69,128]{1,0:T(8,128)S(1)}, f32[69,128]{1,0:T(8,128)S(1)}, u32[]{:S(2)}, u32[]{:S(2)}) collective-permute-start(f32[69,128]{1,0:T(8,128)S(1)} %get-tuple-element.20), channel_id=1, source_target_pairs={{0,31},{1,2},{2,1},{3,4},{4,3},{5,6},{6,5},{7,8},{8,7},{9,10},{10,... | collective-permute-start | bytes 105992 | tf_op jit(solution)/shard_map/ppermute | solution.py:544
  8.6 1.8 %shard_map.113 = (f32[69,80,128]{2,1,0:T(8,128)S(1)}, s32[64,128]{1,0:T(8,128)S(1)}, f32[64,128]{1,0:T(8,128)S(1)}, f32[64,128]{1,0:T(8,128)S(1)}, bf16[64,384]{...) custom-call(f32[69,8192]{1,0:T(8,128)} %coupling.3, s32[64,128]{1,0:T(8,128)} %bitcast.2), custom_call_target="tpu_custom_call" | custom-call | flops 4521984 | bytes 4587520 | tf_op jit(solution)/shard_map/pallas_call | solution.py:29
  10.4 0.0 collective-permute-done.pair_edge
  10.5 0.0 collective-permute-done.1.next_edge
  10.5 0.0 copy-done
  10.5 0.0 copy-start.1
  10.5 0.0 copy-start.2
  10.5 2.4 %shard_map.115 = (f32[68,64,128]{2,1,0:T(8,128)S(1)}, f32[68,64,128]{2,1,0:T(8,128)S(1)}, f32[4,64,128]{2,1,0:T(8,128)S(1)}, f32[2,64,128]{2,1,0:T(8,128)S(1)}, ...) custom-call(f32[69,80,128]{2,1,0:T(8,128)S(1)} %get-tuple-element.18.padded, ...), custom_call_target="tpu_custom_call" | custom-call | flops 11468800 | bytes 1769472 | tf_op jit(solution)/shard_map/pallas_call | solution.py:29
  12.9 10.8 %all_to_all.5.inbox.slots = f32[8,6,8,128]{3,2,1,0:T(8,128)S(1)} all-to-all(f32[8,6,8,128]{3,2,1,0:T(8,128)S(1)} %get-tuple-element.25), channel_id=1, replica_groups=mesh['lon'=8,'lev'=4] {'lon'}, dimensions={0} | all-to-all | bytes 393216 | tf_op jit(solution)/shard_map/all_to_all | solution.py:596
  23.7 0.0 copy-done.1
  23.7 0.0 copy-done.2
  23.7 3.0 %shard_map.116 = (f32[70,8192]{1,0:T(8,128)}, f32[9,8192]{1,0:T(8,128)}) custom-call(f32[8,6,8,128]{3,2,1,0:T(8,128)S(1)} %all_to_all.5.inbox.slots, f32[8,6,8,128]{3,2,1,0:T(8,128)S(1)} %all_to_all.5.inbox.slots, f32[68,64,128]{2,1,0:T(8,128)S(1)} %get-tuple-element.26.offset, f32[68,64,128]{2,1,0:T(8,128)S(1)} %get-tuple-element.27.factor, ...), custom_call_target="tpu_custom_call" | custom-call | flops 2293760 | bytes 2293760 | tf_op jit(solution)/shard_map/pallas_call | solution.py:29
Async XLA Ops:
  1.5 9.0 %copy-start = (f32[70,8192]{1,0:T(8,128)S(1)}, f32[70,8192]{1,0:T(8,128)}, u32[]{:S(2)}) copy-start(f32[70,8192]{1,0:T(8,128)} %old.1) | copy-start | bytes 6881284
  1.5 9.0 %collective-permute-start = (f32[69,128]{1,0:T(8,128)S(1)}, f32[69,128]{1,0:T(8,128)S(1)}, u32[]{:S(2)}, u32[]{:S(2)}) collective-permute-start(f32[69,128]{1,0:T(8,128)S(1)} %get-tuple-element.19), channel_id=1, source_target_pairs={{0,1},{1,0},{2,3},{3,2},{4,5},{5,4},{6,7},{7,6},{8,9},{9,8},{10,11... | collective-permute-start | bytes 105992 | tf_op jit(solution)/shard_map/ppermute | solution.py:545
  2.0 8.4 %collective-permute-start.1 = (f32[69,128]{1,0:T(8,128)S(1)}, f32[69,128]{1,0:T(8,128)S(1)}, u32[]{:S(2)}, u32[]{:S(2)}) collective-permute-start(f32[69,128]{1,0:T(8,128)S(1)} %get-tuple-element.20), channel_id=1, source_target_pairs={{0,31},{1,2},{2,1},{3,4},{4,3},{5,6},{6,5},{7,8},{8,7},{9,10},{10,... | collective-permute-start | bytes 105992 | tf_op jit(solution)/shard_map/ppermute | solution.py:544
  10.5 13.2 %copy-start.1 = (s32[8192]{0:T(1024)S(1)}, s32[8192]{0:T(1024)}, u32[]{:S(2)}) copy-start(s32[8192]{0:T(1024)} %param.13) | copy-start | bytes 98308
  10.5 13.2 %copy-start.2 = (f32[8192]{0:T(1024)S(1)}, f32[8192]{0:T(1024)}, u32[]{:S(2)}) copy-start(f32[8192]{0:T(1024)} %param.12) | copy-start | bytes 98308

commit v6 on v5

--- a/solution.py
+++ b/solution.py
@@ -379,6 +379,7 @@
     tile_temp,
     solved,
     warm,
+    ground_pair,
     column_buffer,
     tile_buffer,
     sems,
@@ -424,8 +425,8 @@
             k, surface, next_flux = update(
                 solved[0, here, :], solved[1, here, :], *(params[n, here, :] for n in range(4)), last
             )
-            column_buffer[0, here, :] = surface
-            column_buffer[1, here, :] = k
+            ground_pair[0, here, :] = surface
+            ground_pair[1, here, :] = k
             fluxes.append(next_flux)
         return fluxes
 
@@ -447,32 +448,32 @@
     width = 2
     parts = blocks // width
 
+    def put(level, g, value):
+        column_buffer[level, pl.ds(g * SUB * LANES, SUB * LANES)] = value.reshape(SUB * LANES)
+
     def solve_columns(part):
-        chosen = spans[part * width : (part + 1) * width]
+        chosen = range(part * width, (part + 1) * width)
         values = []
-        for here in chosen:
-            surface, k = column_buffer[0, here, :], column_buffer[1, here, :]
+        for g in chosen:
+            here = spans[g]
+            surface, k = ground_pair[0, here, :], ground_pair[1, here, :]
             n1, w = params[1, here, :], params[2, here, :]
             value = (n1 + k * surface) * reciprocal(w + k)
-            column_buffer[1, here, :] = value
+            put(0, g, surface)
+            put(1, g, value)
             values.append(value)
-
-        def substitute(level, values):
-            values = [
-                offset[level, here, :] + factor[level, here, :] * value
-                for here, value in zip(chosen, values)
-            ]
-            for here, value in zip(chosen, values):
-                column_buffer[level + 2, here, :] = value
-            return values
-
-        lax.fori_loop(0, upper, substitute, values, unroll=upper // 4)
-        for t in range(part * width * SUB, (part + 1) * width * SUB):
-            pltpu.make_async_copy(
-                column_buffer.at[:, t, :],
-                column_temp.at[:, pl.ds(t * LANES, LANES)],
-                sems.at[part],
-            ).start()
+        for level in range(upper):
+            for n, g in enumerate(chosen):
+                here = spans[g]
+                values[n] = offset[level, here, :] + factor[level, here, :] * values[n]
+                put(level + 2, g, values[n])
+        part_copy(part).start()
+
+    def part_copy(part):
+        area = pl.ds(part * width * SUB * LANES, width * SUB * LANES)
+        return pltpu.make_async_copy(
+            column_buffer.at[:, area], column_temp.at[:, area], sems.at[part]
+        )
 
     lax.fori_loop(0, ITERS, over_columns, [zero] * blocks, unroll=2)
     early = min(2, parts)
@@ -491,8 +492,7 @@
         solve_columns(part)
     pltpu.make_async_copy(tile_buffer, tile_buffer, tile_sem).wait()
     for part in range(parts):
-        span = column_buffer.at[:, pl.ds(part * width * SUB, width * SUB), :]
-        pltpu.make_async_copy(span, span, sems.at[part]).wait()
+        part_copy(part).wait()
 
 
 def on_device(
@@ -615,7 +615,8 @@
         [
             VMEM((2,) + full, F32),
             VMEM(full, F32),
-            VMEM((levels,) + full, F32),
+            VMEM((2,) + full, F32),
+            VMEM((levels, columns), F32),
             VMEM((tiles,) + full, F32),
             DMA((blocks // width,)),
             DMA,

time: 27.1 us -> 26.9 us (level)
  no operation moved by 1% of the time
where the time goes in v6:
time: 26.9 us; the launch traced here: 26.5 us
  blocking collectives  10.8 us (40%)
  Pallas kernels  7.84 us (29%)
  starting transfers between devices  7.14 us (27%)
  between operations  0.7 us (3%)
    all_to_all x1, blocking collectives, on_device(): inbox = lax.all_to_all(send, 'lon', split_axis=0, concat_axis=0, tiled=True)  10.8 us
    pallas_call x4, Pallas kernels, chip_call(): pl.pallas_call(kernel, out_shape=outs, in_specs=[pl.BlockSpec(memory_spac...  7.84 us
    ppermute x1, starting transfers between devices, on_device(): next_edge = lax.ppermute(next_own, axes, following)  6.58 us
    ppermute x1, starting transfers between devices, on_device(): pair_edge = lax.ppermute(pair_own, axes, pairs)  0.56 us
  transfers between devices with their start and end apart: 2, of which 0 were waited for; matrix products, arithmetic and copies ran while one was open for 0% of the time, Pallas kernels for 7%

profile of v6, /device:TPU:0, one launch (start us, length us, event | category | flops | bytes accessed | tf_op | source)
XLA Modules:
  0.0 26.5 jit_solution(9331351070161706181)
XLA Ops:
  0.6 0.8 %shard_map.114 = (f32[69,128]{1,0:T(8,128)S(1)}, f32[69,128]{1,0:T(8,128)S(1)}) custom-call(f32[69,8192]{1,0:T(8,128)} %coupling.3), custom_call_target="tpu_custom_call" | custom-call | bytes 141312 | tf_op jit(solution)/shard_map/pallas_call | solution.py:29
  1.5 0.0 copy-start
  1.5 0.6 %collective-permute-start = (f32[69,128]{1,0:T(8,128)S(1)}, f32[69,128]{1,0:T(8,128)S(1)}, u32[]{:S(2)}, u32[]{:S(2)}) collective-permute-start(f32[69,128]{1,0:T(8,128)S(1)} %get-tuple-element.19), channel_id=1, source_target_pairs={{0,1},{1,0},{2,3},{3,2},{4,5},{5,4},{6,7},{7,6},{8,9},{9,8},{10,11... | collective-permute-start | bytes 105992 | tf_op jit(solution)/shard_map/ppermute | solution.py:545
  2.0 6.6 %collective-permute-start.1 = (f32[69,128]{1,0:T(8,128)S(1)}, f32[69,128]{1,0:T(8,128)S(1)}, u32[]{:S(2)}, u32[]{:S(2)}) collective-permute-start(f32[69,128]{1,0:T(8,128)S(1)} %get-tuple-element.20), channel_id=1, source_target_pairs={{0,31},{1,2},{2,1},{3,4},{4,3},{5,6},{6,5},{7,8},{8,7},{9,10},{10,... | collective-permute-start | bytes 105992 | tf_op jit(solution)/shard_map/ppermute | solution.py:544
  8.6 1.8 %shard_map.113 = (f32[69,80,128]{2,1,0:T(8,128)S(1)}, s32[64,128]{1,0:T(8,128)S(1)}, f32[64,128]{1,0:T(8,128)S(1)}, f32[64,128]{1,0:T(8,128)S(1)}, bf16[64,384]{...) custom-call(f32[69,8192]{1,0:T(8,128)} %coupling.3, s32[64,128]{1,0:T(8,128)} %bitcast.2), custom_call_target="tpu_custom_call" | custom-call | flops 4521984 | bytes 4587520 | tf_op jit(solution)/shard_map/pallas_call | solution.py:29
  10.4 0.0 collective-permute-done.pair_edge
  10.5 0.0 collective-permute-done.1.next_edge
  10.5 0.0 copy-done
  10.5 0.0 copy-start.1
  10.5 0.0 copy-start.2
  10.5 2.4 %shard_map.115 = (f32[68,64,128]{2,1,0:T(8,128)S(1)}, f32[68,64,128]{2,1,0:T(8,128)S(1)}, f32[4,64,128]{2,1,0:T(8,128)S(1)}, f32[2,64,128]{2,1,0:T(8,128)S(1)}, ...) custom-call(f32[69,80,128]{2,1,0:T(8,128)S(1)} %get-tuple-element.18.padded, ...), custom_call_target="tpu_custom_call" | custom-call | flops 11468800 | bytes 1769472 | tf_op jit(solution)/shard_map/pallas_call | solution.py:29
  12.9 10.8 %all_to_all.5.inbox.slots = f32[8,6,8,128]{3,2,1,0:T(8,128)S(1)} all-to-all(f32[8,6,8,128]{3,2,1,0:T(8,128)S(1)} %get-tuple-element.25), channel_id=1, replica_groups=mesh['lon'=8,'lev'=4] {'lon'}, dimensions={0} | all-to-all | bytes 393216 | tf_op jit(solution)/shard_map/all_to_all | solution.py:596
  23.7 0.0 copy-done.1
  23.7 0.0 copy-done.2
  23.7 2.8 %shard_map.116 = (f32[70,8192]{1,0:T(8,128)}, f32[9,8192]{1,0:T(8,128)}) custom-call(f32[8,6,8,128]{3,2,1,0:T(8,128)S(1)} %all_to_all.5.inbox.slots, f32[8,6,8,128]{3,2,1,0:T(8,128)S(1)} %all_to_all.5.inbox.slots, f32[68,64,128]{2,1,0:T(8,128)S(1)} %get-tuple-element.26.offset, f32[68,64,128]{2,1,0:T(8,128)S(1)} %get-tuple-element.27.factor, ...), custom_call_target="tpu_custom_call" | custom-call | flops 2293760 | bytes 2293760 | tf_op jit(solution)/shard_map/pallas_call | solution.py:29
Async XLA Ops:
  1.5 9.0 %copy-start = (f32[70,8192]{1,0:T(8,128)S(1)}, f32[70,8192]{1,0:T(8,128)}, u32[]{:S(2)}) copy-start(f32[70,8192]{1,0:T(8,128)} %old.1) | copy-start | bytes 6881284
  1.5 9.0 %collective-permute-start = (f32[69,128]{1,0:T(8,128)S(1)}, f32[69,128]{1,0:T(8,128)S(1)}, u32[]{:S(2)}, u32[]{:S(2)}) collective-permute-start(f32[69,128]{1,0:T(8,128)S(1)} %get-tuple-element.19), channel_id=1, source_target_pairs={{0,1},{1,0},{2,3},{3,2},{4,5},{5,4},{6,7},{7,6},{8,9},{9,8},{10,11... | collective-permute-start | bytes 105992 | tf_op jit(solution)/shard_map/ppermute | solution.py:545
  2.0 8.4 %collective-permute-start.1 = (f32[69,128]{1,0:T(8,128)S(1)}, f32[69,128]{1,0:T(8,128)S(1)}, u32[]{:S(2)}, u32[]{:S(2)}) collective-permute-start(f32[69,128]{1,0:T(8,128)S(1)} %get-tuple-element.20), channel_id=1, source_target_pairs={{0,31},{1,2},{2,1},{3,4},{4,3},{5,6},{6,5},{7,8},{8,7},{9,10},{10,... | collective-permute-start | bytes 105992 | tf_op jit(solution)/shard_map/ppermute | solution.py:544
  10.5 13.2 %copy-start.1 = (s32[8192]{0:T(1024)S(1)}, s32[8192]{0:T(1024)}, u32[]{:S(2)}) copy-start(s32[8192]{0:T(1024)} %param.13) | copy-start | bytes 98308
  10.5 13.2 %copy-start.2 = (f32[8192]{0:T(1024)S(1)}, f32[8192]{0:T(1024)}, u32[]{:S(2)}) copy-start(f32[8192]{0:T(1024)} %param.12) | copy-start | bytes 98308

commit v7 on v6

--- a/solution.py
+++ b/solution.py
@@ -483,14 +483,13 @@
     for i, here in enumerate(spans):
         surface = jnp.where(land_params(i)[3] > 0.0, warm[here, :], zero)
         for t in range(tiles):
-            tile_buffer[t, here, :] = tile_base[t, here, :] + tile_slope[t, here, :] * surface
-    for t in range(rows):
-        pltpu.make_async_copy(
-            tile_buffer.at[:, t, :], tile_temp.at[:, pl.ds(t * LANES, LANES)], tile_sem
-        ).start()
+            value = tile_base[t, here, :] + tile_slope[t, here, :] * surface
+            tile_buffer[t, pl.ds(i * SUB * LANES, SUB * LANES)] = value.reshape(SUB * LANES)
+    tile_copy = pltpu.make_async_copy(tile_buffer, tile_temp, tile_sem)
+    tile_copy.start()
     for part in range(early, parts):
         solve_columns(part)
-    pltpu.make_async_copy(tile_buffer, tile_buffer, tile_sem).wait()
+    tile_copy.wait()
     for part in range(parts):
         part_copy(part).wait()
 
@@ -617,7 +616,7 @@
             VMEM(full, F32),
             VMEM((2,) + full, F32),
             VMEM((levels, columns), F32),
-            VMEM((tiles,) + full, F32),
+            VMEM((tiles, columns), F32),
             DMA((blocks // width,)),
             DMA,
         ],

time: 26.9 us -> 26.7 us (level)
  no operation moved by 1% of the time
where the time goes in v7:
time: 26.7 us; the launch traced here: 26.3 us
  blocking collectives  10.8 us (40%)
  Pallas kernels  7.64 us (29%)
  starting transfers between devices  7.14 us (27%)
  between operations  0.7 us (3%)
    all_to_all x1, blocking collectives, on_device(): inbox = lax.all_to_all(send, 'lon', split_axis=0, concat_axis=0, tiled=True)  10.8 us
    pallas_call x4, Pallas kernels, chip_call(): pl.pallas_call(kernel, out_shape=outs, in_specs=[pl.BlockSpec(memory_spac...  7.64 us
    ppermute x1, starting transfers between devices, on_device(): next_edge = lax.ppermute(next_own, axes, following)  6.58 us
    ppermute x1, starting transfers between devices, on_device(): pair_edge = lax.ppermute(pair_own, axes, pairs)  0.56 us
  transfers between devices with their start and end apart: 2, of which 0 were waited for; matrix products, arithmetic and copies ran while one was open for 0% of the time, Pallas kernels for 7%

profile of v7, /device:TPU:0, one launch (start us, length us, event | category | flops | bytes accessed | tf_op | source)
XLA Modules:
  0.0 26.3 jit_solution(10756790586962719644)
XLA Ops:
  0.6 0.8 %shard_map.114 = (f32[69,128]{1,0:T(8,128)S(1)}, f32[69,128]{1,0:T(8,128)S(1)}) custom-call(f32[69,8192]{1,0:T(8,128)} %coupling.3), custom_call_target="tpu_custom_call" | custom-call | bytes 141312 | tf_op jit(solution)/shard_map/pallas_call | solution.py:29
  1.5 0.0 copy-start
  1.5 0.6 %collective-permute-start = (f32[69,128]{1,0:T(8,128)S(1)}, f32[69,128]{1,0:T(8,128)S(1)}, u32[]{:S(2)}, u32[]{:S(2)}) collective-permute-start(f32[69,128]{1,0:T(8,128)S(1)} %get-tuple-element.19), channel_id=1, source_target_pairs={{0,1},{1,0},{2,3},{3,2},{4,5},{5,4},{6,7},{7,6},{8,9},{9,8},{10,11... | collective-permute-start | bytes 105992 | tf_op jit(solution)/shard_map/ppermute | solution.py:544
  2.0 6.6 %collective-permute-start.1 = (f32[69,128]{1,0:T(8,128)S(1)}, f32[69,128]{1,0:T(8,128)S(1)}, u32[]{:S(2)}, u32[]{:S(2)}) collective-permute-start(f32[69,128]{1,0:T(8,128)S(1)} %get-tuple-element.20), channel_id=1, source_target_pairs={{0,31},{1,2},{2,1},{3,4},{4,3},{5,6},{6,5},{7,8},{8,7},{9,10},{10,... | collective-permute-start | bytes 105992 | tf_op jit(solution)/shard_map/ppermute | solution.py:543
  8.6 1.8 %shard_map.113 = (f32[69,80,128]{2,1,0:T(8,128)S(1)}, s32[64,128]{1,0:T(8,128)S(1)}, f32[64,128]{1,0:T(8,128)S(1)}, f32[64,128]{1,0:T(8,128)S(1)}, bf16[64,384]{...) custom-call(f32[69,8192]{1,0:T(8,128)} %coupling.3, s32[64,128]{1,0:T(8,128)} %bitcast.2), custom_call_target="tpu_custom_call" | custom-call | flops 4521984 | bytes 4587520 | tf_op jit(solution)/shard_map/pallas_call | solution.py:29
  10.4 0.0 collective-permute-done.pair_edge
  10.5 0.0 collective-permute-done.1.next_edge
  10.5 0.0 copy-done
  10.5 0.0 copy-start.1
  10.5 0.0 copy-start.2
  10.5 2.4 %shard_map.115 = (f32[68,64,128]{2,1,0:T(8,128)S(1)}, f32[68,64,128]{2,1,0:T(8,128)S(1)}, f32[4,64,128]{2,1,0:T(8,128)S(1)}, f32[2,64,128]{2,1,0:T(8,128)S(1)}, ...) custom-call(f32[69,80,128]{2,1,0:T(8,128)S(1)} %get-tuple-element.18.padded, ...), custom_call_target="tpu_custom_call" | custom-call | flops 11468800 | bytes 1769472 | tf_op jit(solution)/shard_map/pallas_call | solution.py:29
  12.9 10.8 %all_to_all.5.inbox.slots = f32[8,6,8,128]{3,2,1,0:T(8,128)S(1)} all-to-all(f32[8,6,8,128]{3,2,1,0:T(8,128)S(1)} %get-tuple-element.25), channel_id=1, replica_groups=mesh['lon'=8,'lev'=4] {'lon'}, dimensions={0} | all-to-all | bytes 393216 | tf_op jit(solution)/shard_map/all_to_all | solution.py:595
  23.7 0.0 copy-done.1
  23.7 0.0 copy-done.2
  23.7 2.6 %shard_map.116 = (f32[70,8192]{1,0:T(8,128)}, f32[9,8192]{1,0:T(8,128)}) custom-call(f32[8,6,8,128]{3,2,1,0:T(8,128)S(1)} %all_to_all.5.inbox.slots, f32[8,6,8,128]{3,2,1,0:T(8,128)S(1)} %all_to_all.5.inbox.slots, f32[68,64,128]{2,1,0:T(8,128)S(1)} %get-tuple-element.26.offset, f32[68,64,128]{2,1,0:T(8,128)S(1)} %get-tuple-element.27.factor, ...), custom_call_target="tpu_custom_call" | custom-call | flops 2293760 | bytes 2293760 | tf_op jit(solution)/shard_map/pallas_call | solution.py:29
Async XLA Ops:
  1.5 9.0 %copy-start = (f32[70,8192]{1,0:T(8,128)S(1)}, f32[70,8192]{1,0:T(8,128)}, u32[]{:S(2)}) copy-start(f32[70,8192]{1,0:T(8,128)} %old.1) | copy-start | bytes 6881284
  1.5 9.0 %collective-permute-start = (f32[69,128]{1,0:T(8,128)S(1)}, f32[69,128]{1,0:T(8,128)S(1)}, u32[]{:S(2)}, u32[]{:S(2)}) collective-permute-start(f32[69,128]{1,0:T(8,128)S(1)} %get-tuple-element.19), channel_id=1, source_target_pairs={{0,1},{1,0},{2,3},{3,2},{4,5},{5,4},{6,7},{7,6},{8,9},{9,8},{10,11... | collective-permute-start | bytes 105992 | tf_op jit(solution)/shard_map/ppermute | solution.py:544
  2.0 8.4 %collective-permute-start.1 = (f32[69,128]{1,0:T(8,128)S(1)}, f32[69,128]{1,0:T(8,128)S(1)}, u32[]{:S(2)}, u32[]{:S(2)}) collective-permute-start(f32[69,128]{1,0:T(8,128)S(1)} %get-tuple-element.20), channel_id=1, source_target_pairs={{0,31},{1,2},{2,1},{3,4},{4,3},{5,6},{6,5},{7,8},{8,7},{9,10},{10,... | collective-permute-start | bytes 105992 | tf_op jit(solution)/shard_map/ppermute | solution.py:543
  10.5 13.2 %copy-start.1 = (s32[8192]{0:T(1024)S(1)}, s32[8192]{0:T(1024)}, u32[]{:S(2)}) copy-start(s32[8192]{0:T(1024)} %param.13) | copy-start | bytes 98308
  10.5 13.2 %copy-start.2 = (f32[8192]{0:T(1024)S(1)}, f32[8192]{0:T(1024)}, u32[]{:S(2)}) copy-start(f32[8192]{0:T(1024)} %param.12) | copy-start | bytes 98308
